TPU v7x, 32 devices: a whole 2x2x4 slice. The times are simulated.
32 devices in a mesh: seq: 4 (over y, x), fsdp: 8 (over z, core).
Axes of the slice: x: 2, y: 2, z: 4, core: 2. Of those that a mesh axis runs over, the one named last changes fastest.
Arguments:
- tokens: bfloat16 [8, 1024, 1536], P('fsdp', 'seq'), may hold values from -6 to 6
- mixing_weight: bfloat16 [1536, 2560], P(('seq', 'fsdp')), may hold values from -0.21875 to 0.21875
- output_weight: bfloat16 [1536, 1536], P(('seq', 'fsdp')), may hold values from -0.625 to 0.625
- norm_gains: bfloat16 [1536, 2], P(('seq', 'fsdp')), may hold values from 0.099609375 to 1.8984375
- expert_gate: bfloat16 [1536, 40, 512], P('fsdp', 'seq'), may hold values from -0.15625 to 0.15625
- expert_up: bfloat16 [1536, 40, 512], P('fsdp', 'seq'), may hold values from -0.15625 to 0.15625
- expert_down: bfloat16 [1536, 40, 512], P('fsdp', 'seq'), may hold values from -1.25 to 1.25
- gate_logits: float32 [8, 1024, 8], P('fsdp'), may hold values from -3 to 3
- routes: int32 [8, 1024, 8], P('fsdp'), may hold values from 0 to 39, all different within a row
- fill_order: int32 [8, 1024], P('fsdp'), may hold values from 0 to 1023, each once within a row
- cotangent: bfloat16 [8, 1024, 1536], P('fsdp', 'seq'), may hold values from -6 to 6
Outputs:
- layer_output: bfloat16 [8, 1024, 1536], P('fsdp', 'seq')
- tokens_gradient: float32 [8, 1024, 1536], P('fsdp', 'seq')
- mixing_gradient: float32 [1536, 2560], P(('seq', 'fsdp'))
- output_gradient: float32 [1536, 1536], P(('seq', 'fsdp'))
- gains_gradient: float32 [1536, 2], P(('seq', 'fsdp'))
- gate_gradient: float32 [1536, 40, 512], P('fsdp', 'seq')
- up_gradient: float32 [1536, 40, 512], P('fsdp', 'seq')
- down_gradient: float32 [1536, 40, 512], P('fsdp', 'seq')
- logits_gradient: float32 [8, 1024, 8], P('fsdp', 'seq')
Inputs may be any that keep to these rules, and one draw needn't show every extreme that they name: `routes`: each token names 8 different experts. `fill_order`: each sequence's row holds each token index of that sequence once.
All inputs are finite; a program needn't handle non-finite values.
Results may differ from a plain program's by a relative error of at most 0.017.
The roundings to bfloat16 on the way count: a program that leaves them out, or rounds other values in their place, can miss the bound.
Values may be sent and summed in bfloat16 or wider, within the bound.
A program may use at most 256 MiB of HBM per device.

v0:
```python
import functools
import math

import jax
import jax.numpy as jnp
import numpy as np
from jax import lax
from jax.experimental import pallas as pl
from jax.experimental.pallas import tpu as pltpu
from jax.sharding import Mesh
from jax.sharding import PartitionSpec as P

D = 1536
HEADS = 24
KV_HEADS = 8
HEAD_DIM = 64
FF = 512
EXPERTS = 40
TOP = 8
QROWS = 256
PAD = 128

epsilon = 1e-05
rope_base = 10000.0
single = jnp.float32
narrow = jnp.bfloat16
MESH = pl.DeviceIdType.MESH


def rotary_tables(positions):
    half_width = HEAD_DIM // 2
    frequency = rope_base ** (-2.0 * jnp.arange(half_width, dtype=single) / HEAD_DIM)
    angles = positions.astype(single)[:, None] * frequency[None, :]
    cos_table = jnp.cos(angles)
    sin_table = jnp.sin(angles)
    return (jnp.concatenate([cos_table, cos_table], 1), jnp.concatenate([sin_table, sin_table], 1))


def softmax_last(logit_rows):
    row_max = jnp.max(logit_rows, axis=-1, keepdims=True)
    exponent = jnp.exp(logit_rows - row_max)
    return exponent / jnp.sum(exponent, axis=-1, keepdims=True)


def swap(value, axis, step, size):
    return lax.ppermute(value, axis, [(i, i ^ step) for i in range(size)])


def dot(left, right, left_dim, right_dim):
    return lax.dot_general(
        left, right, (((left_dim,), (right_dim,)), ((), ())), preferred_element_type=single
    )


def rope(values, cos_row, sin_row):
    width = values.shape[-1]
    lane = lax.broadcasted_iota(jnp.int32, values.shape, 1) % HEAD_DIM
    turned = jnp.where(
        lane < HEAD_DIM // 2,
        -pltpu.roll(values, width - HEAD_DIM // 2, 1),
        pltpu.roll(values, HEAD_DIM // 2, 1),
    )
    return values * cos_row + turned * sin_row


def rope_back(values, cos_row, sin_row):
    width = values.shape[-1]
    lane = lax.broadcasted_iota(jnp.int32, values.shape, 1) % HEAD_DIM
    scaled = values * sin_row
    turned = jnp.where(
        lane < HEAD_DIM // 2,
        pltpu.roll(scaled, width - HEAD_DIM // 2, 1),
        -pltpu.roll(scaled, HEAD_DIM // 2, 1),
    )
    return values * cos_row + turned


def wide(table, width):
    return jnp.concatenate([table] * (width // table.shape[1]), axis=1)


def stacked(ref, at, kv, size):
    group_size = HEADS // KV_HEADS
    return jnp.concatenate(
        [
            ref[at : at + size, (kv * group_size + g) * HEAD_DIM : (kv * group_size + g + 1) * HEAD_DIM]
            for g in range(group_size)
        ],
        axis=0,
    )


def key_scores(keys, queries, at, size):
    scores = dot(keys, queries, 1, 1) * (1.0 / math.sqrt(HEAD_DIM))
    shape = scores.shape
    key_at = lax.broadcasted_iota(jnp.int32, shape, 0)
    query_at = lax.broadcasted_iota(jnp.int32, shape, 1) % size + at
    return jnp.where(key_at <= query_at, scores, -jnp.inf)


def attention_body(
    tok_ref, mix_ref, exit_ref, gain_ref, cos_ref, sin_ref,
    normed_ref, q_ref, k_ref, v_ref, att_ref, log_ref, part_ref,
):
    seq_len = tok_ref.shape[0]
    size = QROWS
    for at in range(0, seq_len, size):
        project_rows(
            at, size, tok_ref[at : at + size], mix_ref[...], gain_ref[0:1],
            cos_ref, sin_ref, normed_ref, q_ref, k_ref, v_ref,
        )
    attend_rows(q_ref, k_ref, v_ref, att_ref, log_ref)
    for at in range(0, seq_len, size):
        part_ref[at : at + size] = dot(att_ref[at : at + size], exit_ref[...], 1, 1).astype(narrow)


def attention_call(tokens_all, mixing_own, exit_own, gains, cos_table, sin_table):
    seq_len = tokens_all.shape[0]
    q_width = exit_own.shape[1]
    k_width = (mixing_own.shape[1] - q_width) // 2
    group_size = HEADS // KV_HEADS
    blocks = k_width // HEAD_DIM * (seq_len // QROWS)
    shape = jax.ShapeDtypeStruct
    return pl.pallas_call(
        attention_body,
        out_shape=[
            shape((seq_len, D), narrow),
            shape((seq_len, q_width), narrow),
            shape((seq_len, k_width), narrow),
            shape((seq_len, k_width), narrow),
            shape((seq_len, q_width), narrow),
            shape((blocks, 1, group_size * QROWS), single),
            shape((seq_len, D), narrow),
        ],
        cost_estimate=pl.CostEstimate(
            flops=2 * seq_len * D * (mixing_own.shape[1] + q_width) + 4 * seq_len**2 * q_width * 4,
            bytes_accessed=seq_len * D * 6, transcendentals=0,
        ),
        name="attention_forward",
    )(tokens_all, mixing_own, exit_own, gains, cos_table, sin_table)


def norm_back(grads, values, gain_row):
    inverse = lax.rsqrt(jnp.mean(values * values, axis=-1, keepdims=True) + epsilon)
    normal = values * inverse
    scaled = grads * gain_row
    back = inverse * (scaled - normal * jnp.mean(scaled * normal, axis=-1, keepdims=True))
    return back, jnp.sum(grads * normal, axis=0, keepdims=True)


def attend_back_rows(out_grad, q_ref, k_ref, v_ref, log_ref, pg_ref, keys_sum, values_sum):
    seq_len, k_width = k_ref.shape
    q_width = q_ref.shape[1]
    size = QROWS
    group_size = HEADS // KV_HEADS
    scale = 1.0 / math.sqrt(HEAD_DIM)
    for kv in range(k_width // HEAD_DIM):
        lanes = slice(kv * HEAD_DIM, (kv + 1) * HEAD_DIM)
        keys_sum[...] = jnp.zeros_like(keys_sum)
        values_sum[...] = jnp.zeros_like(values_sum)
        for block in range(seq_len // size):
            at = block * size
            end = at + size
            queries = stacked(q_ref, at, kv, size)
            grads = stacked(out_grad, at, kv, size)
            keys, values = k_ref[:end, lanes], v_ref[:end, lanes]
            scores = key_scores(keys, queries, at, size)
            soft = jnp.exp(scores - log_ref[kv * (seq_len // size) + block])
            values_sum[:end] += dot(soft.astype(narrow), grads, 1, 0)
            soft_grad = dot(values, grads, 1, 1)
            delta = jnp.sum(soft * soft_grad, axis=0, keepdims=True)
            scores_grad = (soft * (soft_grad - delta)).astype(narrow)
            keys_sum[:end] += dot(scores_grad, queries, 1, 0) * scale
            query_grad = dot(keys, scores_grad, 0, 0) * scale
            for g in range(group_size):
                head = kv * group_size + g
                pg_ref[at:end, head * HEAD_DIM : (head + 1) * HEAD_DIM] = (
                    query_grad[:, g * size : (g + 1) * size].T.astype(narrow)
                )
        first = q_width + kv * HEAD_DIM
        pg_ref[:, first : first + HEAD_DIM] = keys_sum[...].astype(narrow)
        first += k_width
        pg_ref[:, first : first + HEAD_DIM] = values_sum[...].astype(narrow)


def project_back_rows(pg_ref, mix_ref, tok_ref, cos_ref, sin_ref, part_ref, turned, size):
    gain = jnp.zeros((1, D), single)
    for at in range(0, tok_ref.shape[0], size):
        rows = slice(at, at + size)
        pg_ref[rows, :turned] = rope_back(
            pg_ref[rows, :turned].astype(single), wide(cos_ref[rows], turned),
            wide(sin_ref[rows], turned),
        ).astype(narrow)
        normed_part = dot(pg_ref[rows], mix_ref, 1, 1)
        part_ref[rows] = normed_part.astype(narrow)
        values = tok_ref[rows].astype(single)
        inverse = lax.rsqrt(jnp.mean(values * values, axis=-1, keepdims=True) + epsilon)
        gain = gain + jnp.sum(normed_part * (values * inverse), axis=0, keepdims=True)
    return gain


def attention_back_body(
    grad_ref, exit_ref, mix_ref, q_ref, k_ref, v_ref, log_ref, tok_ref, cos_ref, sin_ref,
    pg_ref, part_ref, gain_ref,
    out_grad, keys_sum, values_sum,
):
    size = QROWS
    for at in range(0, tok_ref.shape[0], size):
        out_grad[at : at + size] = dot(grad_ref[at : at + size], exit_ref[...], 1, 0).astype(narrow)
    attend_back_rows(out_grad, q_ref, k_ref, v_ref, log_ref, pg_ref, keys_sum, values_sum)
    turned = q_ref.shape[1] + k_ref.shape[1]
    gain_ref[...] = project_back_rows(
        pg_ref, mix_ref[...], tok_ref, cos_ref, sin_ref, part_ref, turned, size
    )


def totals(wire, t, first, third, zed, buffers, out_send, own_out, half_out):
    sources = (first, third, zed)
    for g in (1, 0):
        loads = [wire.near(ref.at[g], buffers.at[i]) for i, ref in enumerate(sources)]
        for load in loads:
            load.wait()
        total = buffers[0].astype(single) + buffers[1].astype(single) + buffers[2].astype(single)
        if g:
            out_send[...] = total.astype(narrow)
            wire.go(out_send, half_out, wire.to_half)
        else:
            buffers[0] = total.astype(narrow)
            wire.near(buffers.at[0], own_out).wait()


def backward_body(
    ba_ref, bo_ref, oa_ref, oo_ref, pickall_ref, tokall_ref, gg_ref, gu_ref, gd_ref,
    hid_ref, gain_ref, cot_ref, wall_ref, q_ref, k_ref, v_ref, log_ref, cos_ref, sin_ref,
    slot_ref, table_ref, otab_ref,
    pg_ref, part_ref, gsum_ref, hgrad_ref, layer_ref, lgrad_ref,
    ra_ref, mo_ref, ma_ref, grad_out, c1_ref, c3_ref, zb_ref, own_ref, hx_ref,
    ag, out_grad, keys_sum, values_sum, land_a, land_b, land_h, land_m, sums, own_rows, buffers, far,
    leave, passed, passing, values, pick, stage, route_own, route_send, land_r, quarters, land_q, logits,
    send, recv, local,
):
    wire = Wire(send, recv, local)
    s, groups = wire.s, wire.groups
    size = hid_ref.shape[0]
    q_width, k_width = q_ref.shape[1], k_ref.shape[1]
    mix_width = q_width + 2 * k_width
    terms = (gg_ref, gu_ref, gd_ref)
    wire.meet()

    middle = size // 2

    def scatter(source, landing):
        return wire.scatter(lambda j: source.at[s ^ j], landing)

    def scatter_on(keys, source, landing, which):
        loads = [
            wire.near(source.at[s ^ 2, pl.ds(0, middle)], passed.at[0]),
            wire.near(source.at[s ^ 1, pl.ds(middle, middle)], passed.at[1]),
        ]
        for load in loads:
            load.wait()
        wire.scatter_on(
            keys, landing, lambda j: passed[0 if j == 2 else 1].astype(single), passing.at[which]
        )

    def quarter_sends(source, landing):
        return [
            wire.go(source.at[s ^ j], landing.at[j - 1], wire.to_seq[j]) for j in range(1, groups)
        ]

    def fetch(source, b):
        loads = [wire.near(source, values)]
        if b is not None:
            loads.append(wire.near(pickall_ref.at[b], pick))
        for load in loads:
            load.wait()

    def combine(j):
        return dot(pick[:, j * size : (j + 1) * size], values[...], 0, 0).astype(narrow)

    def combine_out(target):
        for j in range(groups):
            stage[j] = combine(j)
        wire.near(stage, target).wait()

    core_go = []
    for t in range(3):
        core_go.append(
            (
                wire.go(terms[t].at[3], c3_ref.at[t], wire.to_core),
                wire.go(terms[t].at[1], c1_ref.at[t], wire.to_core),
            )
        )
    fetch(bo_ref, 1)
    combine_out(mo_ref)
    other_go = scatter(mo_ref, land_a)
    own_rows[0] = stage[s]
    z_go = []

    def send_far(t):
        wire.come(core_go[t][0])
        if t >= 2:
            wire.leave(z_go[t - 2])
        for g in (1, 0):
            loads = [
                wire.near(terms[t].at[2, g], buffers.at[0]),
                wire.near(c3_ref.at[t, g], buffers.at[1]),
            ]
            for load in loads:
                load.wait()
            far[t % 2, g] = (buffers[0].astype(single) + buffers[1].astype(single)).astype(narrow)
        z_go.append(wire.go(far.at[t % 2], zb_ref.at[t], wire.to_z))

    send_far(0)
    fetch(ba_ref, 0)
    combine_out(ra_ref)
    own_go = scatter(ra_ref, land_b)
    own_rows[1] = stage[s]
    scatter_on(other_go, mo_ref, land_a, 0)

    own_count = slot_ref.shape[0]
    slots = slot_ref.shape[1] // 2
    ids = own_ids(own_count, 2 * own_count)

    def route_rows(b, table):
        total = jnp.zeros((TOP, groups * size), single)
        for e in range(own_count):
            mine = pick[e * slots : (e + 1) * slots].astype(single)
            row = jnp.sum(mine * slot_ref[e, b * slots : (b + 1) * slots], axis=0, keepdims=True)
            total = total + jnp.where(table[0:TOP] == ids[e], row, 0.0)
        return total

    route_own[...] = route_rows(0, table_ref)
    fetch(oa_ref, None)
    combine_out(ma_ref)
    own_rows[3] = stage[s]
    total = wire.scatter_end(other_go, land_a, own_rows[0].astype(single))
    sums[...] = total.astype(narrow)
    half_go = wire.go(sums, land_h, wire.to_half)
    scatter_on(own_go, ra_ref, land_b, 1)
    send_far(1)
    for k in other_go:
        wire.leave(k)
    fetch(oo_ref, 1)
    combine_out(mo_ref)
    own_rows[2] = stage[s]
    route_send[...] = route_rows(1, otab_ref)
    route_go = wire.go(route_send, land_r, wire.to_half)
    total = wire.scatter_end(own_go, land_b, own_rows[1].astype(single))
    wire.come(half_go)
    total = total + land_h[...].astype(single)
    back, gain_two = norm_back(total, hid_ref[...], gain_ref[1:2])
    hidden_grad = cot_ref[...].astype(single) + back
    hgrad_ref[...] = hidden_grad
    ag[s] = hidden_grad.astype(narrow)
    grad_go = wire.gather(ag.at[s], ag)
    wire.come(route_go)
    total = route_own[...] + land_r[...]
    for j in range(groups):
        quarters[j] = total[:, j * size : (j + 1) * size]
        logits[j] = table_ref[TOP : 2 * TOP, j * size : (j + 1) * size]
    quarter_go = quarter_sends(quarters, land_q)

    def finish_term(t):
        wire.come(core_go[t][1], z_go[t])
        totals(
            wire, t, terms[t].at[0], c1_ref.at[t], zb_ref.at[t], buffers, leave.at[t],
            own_ref.at[t], hx_ref.at[t],
        )

    finish_term(0)
    wire.gather_on(grad_go, ag)
    send_far(2)
    tok_rows = values.at[pl.ds(0, groups * size)]
    load_tok = wire.near(tokall_ref, tok_rows)
    wire.gather_end(grad_go)
    moe_go = scatter(mo_ref, land_a)
    moe_own_go = scatter(ma_ref, land_b)
    keep_grad = wire.near(ag, grad_out)
    exit_own = wall_ref[:, mix_width : mix_width + q_width]
    for j in range(groups):
        out_grad[j * size : (j + 1) * size] = dot(ag[j], exit_own, 1, 0).astype(narrow)
    attend_back_rows(out_grad, q_ref, k_ref, v_ref, log_ref, pg_ref, keys_sum, values_sum)
    for k in other_go[4:] + own_go[4:]:
        wire.leave(k)
    scatter_on(moe_go, mo_ref, land_a, 0)
    scatter_on(moe_own_go, ma_ref, land_b, 1)
    finish_term(1)
    load_tok.wait()
    gain_one = project_back_rows(
        pg_ref, wall_ref[:, :mix_width], tok_rows, cos_ref, sin_ref, part_ref, q_width + k_width, size
    )
    gsum_ref[...] = jnp.concatenate([gain_one, gain_two, jnp.zeros((6, D), single)], axis=0)
    total = wire.scatter_end(moe_go, land_a, own_rows[2].astype(single))
    wire.leave(half_go)
    sums[...] = total.astype(narrow)
    moe_half_go = wire.go(sums, land_m, wire.to_half)
    wire.come(*quarter_go)
    route_grad = quarters[s]
    for j in range(groups - 1):
        route_grad = route_grad + land_q[j]
    top = logits[s]
    exponent = jnp.exp(top - jnp.max(top, axis=0, keepdims=True))
    gating = exponent / jnp.sum(exponent, axis=0, keepdims=True)
    lgrad_ref[...] = gating * (route_grad - jnp.sum(gating * route_grad, axis=0, keepdims=True))
    total = wire.scatter_end(moe_own_go, land_b, hid_ref[...] + own_rows[3].astype(single))
    wire.come(moe_half_go)
    layer_ref[...] = (total + land_m[...].astype(single)).astype(narrow)
    keep_grad.wait()
    wire.finish()


def backward_call(
    backs, outs, pick, terms, hidden, gains, cot, wall, q, k, v, logs, tokens_all,
    cos_table, sin_table, slot_grad, table, other_table,
):
    size = hidden.shape[0]
    seq_len = tokens_all.shape[0]
    groups = seq_len // size
    rings, halves, own, part, width = terms[0].shape
    slot_rows = pick.shape[1]
    shape = jax.ShapeDtypeStruct
    vmem = pl.BlockSpec(memory_space=pltpu.VMEM)
    hbm = pl.BlockSpec(memory_space=pl.ANY)
    block = (groups, size, D)
    mix_width = q.shape[1] + 2 * k.shape[1]
    landing = pltpu.VMEM((6, size // 2, D), narrow)
    route = pltpu.VMEM((TOP, seq_len), single)
    count = 72
    return pl.pallas_call(
        backward_body,
        in_specs=[hbm] * 9 + [vmem] * 13,
        out_specs=[vmem] * 6 + [hbm] * 9,
        out_shape=[
            shape((seq_len, mix_width), narrow),
            shape((seq_len, D), narrow),
            shape((8, D), single),
            shape((size, D), single),
            shape((size, D), narrow),
            shape((TOP, size), single),
            shape(block, narrow),
            shape(block, narrow),
            shape(block, narrow),
            shape(block, narrow),
            shape((3, halves, own, part, width), narrow),
            shape((3, halves, own, part, width), narrow),
            shape((3, halves, own, part, width), narrow),
            shape((2, own, part, width), narrow),
            shape((2, own, part, width), narrow),
        ],
        scratch_shapes=[
            pltpu.VMEM(block, narrow),
            pltpu.VMEM(q.shape, narrow),
            pltpu.VMEM((seq_len, HEAD_DIM), single),
            pltpu.VMEM((seq_len, HEAD_DIM), single),
            landing,
            landing,
            pltpu.VMEM((size, D), narrow),
            pltpu.VMEM((size, D), narrow),
            pltpu.VMEM((size, D), narrow),
            pltpu.VMEM((4, size, D), narrow),
            pltpu.VMEM((3, own, part, width), narrow),
            pltpu.VMEM((2, halves, own, part, width), narrow),
            pltpu.VMEM((2, own, part, width), narrow),
            pltpu.VMEM((2, size // 2, D), narrow),
            pltpu.VMEM((2, 2, size // 2, D), narrow),
            pltpu.VMEM((slot_rows, D), narrow),
            pltpu.VMEM((slot_rows, seq_len), narrow),
            pltpu.VMEM(block, narrow),
            route,
            route,
            route,
            pltpu.VMEM((groups, TOP, size), single),
            pltpu.VMEM((groups - 1, TOP, size), single),
            pltpu.VMEM((groups, TOP, size), single),
            pltpu.SemaphoreType.DMA((count,)),
            pltpu.SemaphoreType.DMA((count,)),
            pltpu.SemaphoreType.DMA((count,)),
        ],
        compiler_params=pltpu.CompilerParams(
            collective_id=1, has_side_effects=True, vmem_limit_bytes=67_000_000
        ),
        cost_estimate=pl.CostEstimate(
            flops=150_000_000_000, bytes_accessed=100_000_000, transcendentals=0
        ),
        name="backward_exchange",
    )(
        *backs, *outs, pick, tokens_all, *terms, hidden, gains, cot, wall, q, k, v, logs,
        cos_table, sin_table, slot_grad, table, other_table,
    )


def final_body(
    part_ref, gd_ref, c1_ref, zb_ref, grad_ref,
    normed_ref, pg_ref, att_ref, gsum_ref, gain_ref, hgrad_ref, tok_ref,
    tgrad_ref, attn_ref, own_ref, hx_ref,
    gw, r1, r2, r3, a2, a6, c4, fin, land_a, passed, passing, own_rows, agv, buffers, leave,
    send, recv, local,
):
    wire = Wire(send, recv, local)
    s, f, groups = wire.s, wire.f, wire.groups
    _, shards, few, width = gw.shape
    depth = groups * shards * few
    wire.meet()

    norm_go = wire.scatter(lambda j: part_ref.at[s ^ j], land_a)
    load_grad = wire.near(grad_ref, agv)
    middle = land_a.shape[1]
    loads = [
        wire.near(part_ref.at[s], own_rows),
        wire.near(part_ref.at[s ^ 2, pl.ds(0, middle)], passed.at[0]),
        wire.near(part_ref.at[s ^ 1, pl.ds(middle, middle)], passed.at[1]),
    ]
    totals(
        wire, 2, gd_ref.at[0], c1_ref.at[2], zb_ref.at[2], buffers, leave, own_ref, hx_ref
    )
    mix_width, q_width = pg_ref.shape[1], att_ref.shape[1]
    last = mix_width + q_width
    load_grad.wait()
    shape = (groups, shards, few)
    gw[:, :, :, :mix_width] = (
        dot(normed_ref[...], pg_ref[...], 0, 0).astype(narrow).reshape(shape + (mix_width,))
    )
    grads = agv[...].reshape(groups * agv.shape[1], D)
    gw[:, :, :, mix_width:last] = (
        dot(grads, att_ref[...], 0, 0).astype(narrow).reshape(shape + (q_width,))
    )
    gains = jnp.concatenate([gsum_ref[...], jnp.zeros((width - last - 8, D), single)], axis=0)
    gw[:, :, :, last:] = gains.T.astype(narrow).reshape(shape + (width - last,))
    core_go = [wire.go(gw.at[:, f ^ (m + 1)], r1.at[m // 2], wire.to_core) for m in (2, 6, 0, 4)]
    for load in loads:
        load.wait()
    wire.scatter_on(
        norm_go, land_a, lambda j: passed[0 if j == 2 else 1].astype(single), passing
    )
    wire.come(*core_go)

    def pair_sum(m):
        return gw[:, f ^ m].astype(single) + r1[m // 2].astype(single)

    a2[...] = pair_sum(2).astype(narrow)
    go_2 = wire.go(a2, r2.at[0], wire.to_z)
    a6[...] = pair_sum(6).astype(narrow)
    go_6 = wire.go(a6, r2.at[1], wire.to_z)
    wire.come(go_6)
    c4[...] = (pair_sum(4) + r2[1].astype(single)).astype(narrow)
    go_4 = wire.go(c4, r3, wire.to_half)
    total = wire.scatter_end(norm_go, land_a, own_rows[...].astype(single))
    back, _ = norm_back(total, tok_ref[...].astype(single), gain_ref[0:1])
    tgrad_ref[...] = hgrad_ref[...] + back
    wire.come(go_2, go_4)
    fin[...] = pair_sum(0) + r2[0].astype(single) + r3[...].astype(single)
    attn_ref[s] = fin[s]
    last_go = [wire.go(fin.at[s ^ j], attn_ref.at[s], wire.to_seq[j]) for j in range(1, groups)]
    wire.finish()


def final_call(part, term, c1, zb, grad_all, normed, pg, att, gsum, gains, hgrad, tok, few, width):
    size = tok.shape[0]
    seq_len = normed.shape[0]
    groups = seq_len // size
    _, halves, own, rows, units = term.shape
    shape = jax.ShapeDtypeStruct
    vmem = pl.BlockSpec(memory_space=pltpu.VMEM)
    hbm = pl.BlockSpec(memory_space=pl.ANY)
    block = (groups, size, D)
    slab = (groups, few, width)
    landing = pltpu.VMEM((6, size // 2, D), narrow)
    count = 32
    return pl.pallas_call(
        final_body,
        in_specs=[hbm] * 5 + [vmem] * 7,
        out_specs=[vmem] * 2 + [hbm] * 2,
        out_shape=[
            shape((size, D), single),
            shape(slab, single),
            shape((own, rows, units), narrow),
            shape((own, rows, units), narrow),
        ],
        scratch_shapes=[
            pltpu.VMEM((groups, 8, few, width), narrow),
            pltpu.VMEM((4,) + slab, narrow),
            pltpu.VMEM((2,) + slab, narrow),
            pltpu.VMEM(slab, narrow),
            pltpu.VMEM(slab, narrow),
            pltpu.VMEM(slab, narrow),
            pltpu.VMEM(slab, narrow),
            pltpu.VMEM(slab, single),
            landing,
            pltpu.VMEM((2, size // 2, D), narrow),
            pltpu.VMEM((2, size // 2, D), narrow),
            pltpu.VMEM((size, D), narrow),
            pltpu.VMEM(block, narrow),
            pltpu.VMEM((3, own, rows, units), narrow),
            pltpu.VMEM((own, rows, units), narrow),
            pltpu.SemaphoreType.DMA((count,)),
            pltpu.SemaphoreType.DMA((count,)),
            pltpu.SemaphoreType.DMA((count,)),
        ],
        compiler_params=pltpu.CompilerParams(collective_id=2, has_side_effects=True),
        cost_estimate=pl.CostEstimate(
            flops=50_000_000_000, bytes_accessed=100_000_000, transcendentals=0
        ),
        name="final_exchange",
    )(
        part.reshape(block), term, c1, zb, grad_all, normed, pg, att, gsum, gains, hgrad, tok,
    )


def attention_back_call(grads, exit_own, mixing_own, q, k, v, logs, tokens_all, cos_table, sin_table):
    seq_len = tokens_all.shape[0]
    shape = jax.ShapeDtypeStruct
    return pl.pallas_call(
        attention_back_body,
        out_shape=[
            shape((seq_len, mixing_own.shape[1]), narrow),
            shape((seq_len, D), narrow),
            shape((1, D), single),
        ],
        scratch_shapes=[
            pltpu.VMEM(q.shape, narrow),
            pltpu.VMEM((seq_len, HEAD_DIM), single),
            pltpu.VMEM((seq_len, HEAD_DIM), single),
        ],
        cost_estimate=pl.CostEstimate(
            flops=2 * seq_len * D * (mixing_own.shape[1] + q.shape[1])
            + 10 * seq_len**2 * q.shape[1] * 4,
            bytes_accessed=seq_len * D * 8, transcendentals=0,
        ),
        name="attention_backward",
    )(grads, exit_own, mixing_own, q, k, v, logs, tokens_all, cos_table, sin_table)


def project_rows(at, size, tok_rows, mix, gain_row, cos_ref, sin_ref, normed_ref, q_ref, k_ref, v_ref):
    rows = slice(at, at + size)
    q_width, k_width = q_ref.shape[1], k_ref.shape[1]
    values = tok_rows.astype(single)
    inverse = lax.rsqrt(jnp.mean(values * values, axis=-1, keepdims=True) + epsilon)
    normed = (values * inverse * gain_row).astype(narrow)
    normed_ref[rows] = normed
    projected = dot(normed, mix, 1, 0)
    width = q_width + k_width
    turned = rope(
        projected[:, :width], wide(cos_ref[rows], width), wide(sin_ref[rows], width)
    ).astype(narrow)
    q_ref[rows] = turned[:, :q_width]
    k_ref[rows] = turned[:, q_width:]
    v_ref[rows] = projected[:, width:].astype(narrow)


def attend_rows(q_ref, k_ref, v_ref, att_ref, log_ref):
    seq_len, k_width = k_ref.shape
    size = QROWS
    group_size = HEADS // KV_HEADS
    for kv in range(k_width // HEAD_DIM):
        lanes = slice(kv * HEAD_DIM, (kv + 1) * HEAD_DIM)
        for block in range(seq_len // size):
            at = block * size
            end = at + size
            queries = stacked(q_ref, at, kv, size)
            scores = key_scores(k_ref[:end, lanes], queries, at, size)
            top = jnp.max(scores, axis=0, keepdims=True)
            exponent = jnp.exp(scores - top)
            total = jnp.sum(exponent, axis=0, keepdims=True)
            soft = (exponent * (1.0 / total)).astype(narrow)
            log_ref[kv * (seq_len // size) + block] = top + jnp.log(total)
            out = dot(v_ref[:end, lanes], soft, 0, 0)
            for g in range(group_size):
                head = kv * group_size + g
                att_ref[at:end, head * HEAD_DIM : (head + 1) * HEAD_DIM] = (
                    out[:, g * size : (g + 1) * size].T.astype(narrow)
                )


class Wire:
    def __init__(self, send, recv, local):
        self.send, self.recv, self.local = send, recv, local
        self.remotes, self.landed, self.left, self.locals = [], [], [], 0
        s, h, r = lax.axis_index("seq"), lax.axis_index("half"), lax.axis_index("ring")
        groups = lax.axis_size("seq")
        self.s, self.h, self.r, self.f, self.groups = s, h, r, h * 4 + r, groups
        self.to_half, self.to_z, self.to_core = {"half": h ^ 1}, {"ring": r ^ 2}, {"ring": r ^ 1}
        self.to_seq = [{"seq": s ^ j} for j in range(groups)]

    def meet(self):
        barrier = pltpu.get_barrier_semaphore()
        peers = self.to_seq[1:] + [self.to_half, self.to_z, self.to_core]
        for peer in peers:
            pl.semaphore_signal(barrier, inc=1, device_id=peer, device_id_type=MESH)
        pl.semaphore_wait(barrier, len(peers))

    def go(self, source, target, peer):
        k = len(self.remotes)
        copy = pltpu.make_async_remote_copy(
            src_ref=source, dst_ref=target, send_sem=self.send.at[k], recv_sem=self.recv.at[k],
            device_id=peer, device_id_type=MESH,
        )
        copy.start()
        self.remotes.append(copy)
        self.landed.append(False)
        self.left.append(False)
        return k

    def by_core(self, *sends):
        keys = []
        made = []
        for source, target, peer in sends:
            k = len(self.remotes)
            copy = pltpu.make_async_remote_copy(
                src_ref=source, dst_ref=target, send_sem=self.send.at[k],
                recv_sem=self.recv.at[k], device_id=peer, device_id_type=MESH,
            )
            self.remotes.append(copy)
            self.landed.append(False)
            self.left.append(False)
            keys.append(k)
            made.append(copy)

        @pl.when(self.r % 2 == 0)
        def _():
            for copy in made:
                copy.start()

        @pl.when(self.r % 2 == 1)
        def _():
            for copy in reversed(made):
                copy.start()

        return keys

    def come(self, *which):
        for k in which:
            self.remotes[k].wait_recv()
            self.landed[k] = True

    def leave(self, k):
        if not self.left[k]:
            self.remotes[k].wait_send()
        self.left[k] = True

    def near(self, source, target):
        copy = pltpu.make_async_copy(source, target, self.local.at[self.locals])
        self.locals += 1
        copy.start()
        return copy

    def gather(self, source, target):
        s = self.s
        return [self.go(source, target.at[s], self.to_seq[j]) for j in (1, 2)]

    def gather_on(self, keys, target):
        s, middle = self.s, target.shape[1] // 2
        first, second = pl.ds(0, middle), pl.ds(middle, middle)
        self.come(keys[0])
        block = target.at[s ^ 1, first]
        keys.append(self.go(block, block, self.to_seq[2]))
        self.come(keys[1])
        block = target.at[s ^ 2, second]
        keys.append(self.go(block, block, self.to_seq[1]))

    def gather_end(self, keys):
        self.come(*keys[2:])

    def scatter(self, source, landing):
        middle = landing.shape[1]
        first, second = pl.ds(0, middle), pl.ds(middle, middle)
        return [
            self.go(source(3).at[first], landing.at[1], self.to_seq[1]),
            self.go(source(3).at[second], landing.at[3], self.to_seq[2]),
            self.go(source(1).at[first], landing.at[0], self.to_seq[1]),
            self.go(source(2).at[second], landing.at[2], self.to_seq[2]),
        ]

    def scatter_on(self, keys, landing, kept, passing):
        self.come(keys[0])
        passing[0] = (kept(2) + landing[1].astype(single)).astype(narrow)
        keys.append(self.go(passing.at[0], landing.at[4], self.to_seq[2]))
        self.come(keys[1])
        passing[1] = (kept(1) + landing[3].astype(single)).astype(narrow)
        keys.append(self.go(passing.at[1], landing.at[5], self.to_seq[1]))

    def scatter_end(self, keys, landing, own):
        self.come(*keys[2:])
        first = landing[0].astype(single) + landing[4].astype(single)
        second = landing[2].astype(single) + landing[5].astype(single)
        return own + jnp.concatenate([first, second], axis=0)

    def finish(self):
        for k, copy in enumerate(self.remotes):
            if not self.left[k]:
                copy.wait_send()
            if not self.landed[k]:
                copy.wait_recv()


def place_rows(table, ids, capacity, slots, pick_ref, share_ref, b):
    length = table.shape[1]
    picked, logits, order = table[0:TOP], table[TOP : 2 * TOP], table[2 * TOP : 2 * TOP + 1]
    exponent = jnp.exp(logits - jnp.max(logits, axis=0, keepdims=True))
    gating = exponent / jnp.sum(exponent, axis=0, keepdims=True)
    down = lax.broadcasted_iota(jnp.int32, (length, length), 0).astype(single)
    along = lax.broadcasted_iota(jnp.int32, (length, length), 1).astype(single)
    place_col = jnp.sum(jnp.where(order == down, along, 0.0), axis=1, keepdims=True)
    place_row = jnp.broadcast_to(place_col, (length, 128)).T[0:1]
    earlier = (place_col < place_row).astype(single).astype(narrow)
    hits = [jnp.sum((picked == i).astype(single), axis=0, keepdims=True) for i in ids]
    share = [
        jnp.sum(jnp.where(picked == i, gating, 0.0), axis=0, keepdims=True) for i in ids
    ]
    spare = jnp.zeros((8 - len(ids), length), single)
    rank = dot(jnp.concatenate(hits + [spare], axis=0).astype(narrow), earlier, 1, 0)
    slot_at = lax.broadcasted_iota(jnp.int32, (slots, length), 0).astype(single)
    for e in range(len(ids)):
        kept = (hits[e] > 0.0) & (rank[e : e + 1] < capacity)
        filled = jnp.where(kept, rank[e : e + 1], -1.0) == slot_at
        pick_ref[b, e * slots : (e + 1) * slots] = filled.astype(single).astype(narrow)
        share_ref[e, b * slots : (b + 1) * slots] = jnp.sum(
            jnp.where(filled, share[e], 0.0), axis=1, keepdims=True
        )


def own_ids(own, local_count):
    first = lax.axis_index("seq") * local_count + lax.axis_index("half") * own
    return [(first + e).astype(single) for e in range(own)]


def forward_body(
    tok_ref, pack_ref, cot_ref, wg_ref, wu_ref, wd_ref, cos_ref, sin_ref, table_ref,
    normed_ref, q_ref, k_ref, v_ref, att_ref, log_ref, hid_ref, gain_ref, share_ref, otab_ref,
    tokall_ref, wall_ref, pickall_ref, xa_ref, xo_ref, ya_ref, yo_ref, wout_ref,
    xown_ref, xother_ref, yown_ref, yother_ref,
    tokv, wv, part, landed, passing, xv, other_table, pick, picked_rows, send, recv, local,
):
    wire = Wire(send, recv, local)
    s, h, r, f, groups = wire.s, wire.h, wire.r, wire.f, wire.groups
    _, fsdp, few, width = wv.shape
    q_width, k_width = q_ref.shape[1], k_ref.shape[1]
    mix_width = q_width + 2 * k_width
    size = tok_ref.shape[0]
    middle = size // 2
    wire.meet()

    pack_go = [wire.go(pack_ref.at[s ^ j], wv.at[s, f], wire.to_seq[j]) for j in range(1, groups)]
    tok_go = wire.gather(tok_ref, tokv)
    table_go = wire.go(table_ref, other_table, wire.to_half)
    own_cot = wire.near(cot_ref, ya_ref.at[s])
    wv[s, f] = pack_ref[s]
    tokv[s] = tok_ref[...]

    sources = (wg_ref, wu_ref, wd_ref)

    def weights_first(t):
        own, other = sources[t].at[h], sources[t].at[1 - h]
        target = wout_ref.at[t, h, r]
        keys = wire.by_core((other, target, wire.to_half), (own, target, wire.to_z))
        wire.go(own, target, wire.to_core)
        return keys

    def weights_next(t, keys):
        wire.come(keys[0])
        came = wout_ref.at[t, 1 - h, r]
        on_z = wire.go(came, came, wire.to_z)
        wire.go(came, came, wire.to_core)
        wire.come(keys[1])
        beside = wout_ref.at[t, h, r ^ 2]
        wire.go(beside, beside, wire.to_core)
        return on_z

    def weights_last(t, key):
        wire.come(key)
        beyond = wout_ref.at[t, 1 - h, r ^ 2]
        wire.go(beyond, beyond, wire.to_core)

    wire.come(*pack_go)
    mine = wv.at[:, f]
    a_half = wire.go(mine, mine, wire.to_half)
    a_z = wire.go(mine, mine, wire.to_z)
    parts_go = [wire.go(mine, mine, wire.to_core)]
    wire.come(a_half)
    block = wv.at[:, f ^ 4]
    b_z = wire.go(block, block, wire.to_z)
    parts_go.append(wire.go(block, block, wire.to_core))
    wire.come(a_z)
    block = wv.at[:, f ^ 2]
    parts_go.append(wire.go(block, block, wire.to_core))
    cot_half = wire.go(cot_ref, yo_ref.at[s], wire.to_half)
    gate_first = weights_first(0)
    wire.gather_on(tok_go, tokv)
    cot_go = wire.gather(cot_ref, ya_ref)
    wire.come(b_z)
    block = wv.at[:, f ^ 6]
    parts_go.append(wire.go(block, block, wire.to_core))
    up_first = weights_first(1)

    own, slots = wout_ref.shape[3], share_ref.shape[1] // 2
    capacity = (groups * size * TOP + EXPERTS - 1) // EXPERTS
    ids = own_ids(own, 2 * own)
    place_rows(table_ref[...], ids, capacity, slots, pick, share_ref, 0)
    wire.gather_end(tok_go)
    wire.come(*parts_go)
    wire.gather_on(cot_go, ya_ref)
    keep_tok = wire.near(tokv, tokall_ref)
    keep_wall = wire.near(wv, wall_ref)
    depth = groups * fsdp * few
    gains = wv[:, :, :, mix_width + q_width :].reshape(depth, width - mix_width - q_width)
    gains = gains.astype(single).T[0:8]
    gain_ref[...] = gains
    for j in range(groups):
        project_rows(
            j * size, size, tokv[j], wv[:, :, :, :mix_width].reshape(depth, mix_width),
            gains[0:1], cos_ref, sin_ref, normed_ref, q_ref, k_ref, v_ref,
        )
    attend_rows(q_ref, k_ref, v_ref, att_ref, log_ref)
    exit_own = wv[:, :, :, mix_width : mix_width + q_width].reshape(depth, q_width)
    for j in (3, 1, 2, 0):
        rows = pl.ds(pl.multiple_of((s ^ j) * size, size), size)
        partial = dot(att_ref[rows], exit_own, 1, 1)
        if j:
            part[j - 1] = partial.astype(narrow)
        else:
            part_go = wire.scatter(lambda j: part.at[j - 1], landed)
            hid_ref[...] = tok_ref[...].astype(single) + partial

    def dispatch(b, source, target):
        wire.near(source, tokv).wait()
        whole = tokv[...].reshape(groups * size, D)
        for at in range(0, D, 512):
            picked_rows[:, at : at + 512] = dot(pick[b], whole[:, at : at + 512], 1, 0).astype(narrow)
        wire.near(picked_rows, target).wait()

    def kept(j):
        return part[j - 1, (0 if j == 2 else middle) : (middle if j == 2 else size)].astype(single)

    for k in tok_go[2:]:
        wire.leave(k)
    gate_next = weights_next(0, gate_first)
    wire.scatter_on(part_go, landed, kept, passing)
    keep_tok.wait()
    own_cot.wait()
    wire.gather_end(cot_go)
    dispatch(0, ya_ref, yown_ref)
    hidden = wire.scatter_end(part_go, landed, hid_ref[...])
    hid_ref[...] = hidden
    inverse = lax.rsqrt(jnp.mean(hidden * hidden, axis=-1, keepdims=True) + epsilon)
    xv[...] = (hidden * inverse * gains[1:2]).astype(narrow)
    row_half = wire.go(xv, xo_ref.at[s], wire.to_half)
    row_go = wire.gather(xv, xa_ref)
    own_row = wire.near(xv, xa_ref.at[s])
    down_first = weights_first(2)
    wire.come(table_go)
    otab_ref[...] = other_table[...]
    place_rows(other_table[...], ids, capacity, slots, pick, share_ref, 1)
    keep_pick = wire.near(pick, pickall_ref)
    wire.gather_on(row_go, xa_ref)
    wire.come(cot_half)
    up_next = weights_next(1, up_first)
    wire.come(row_half)
    other_go = wire.gather(xo_ref.at[s], xo_ref)
    cot_other = wire.gather(yo_ref.at[s], yo_ref)
    weights_last(0, gate_next)
    own_row.wait()
    wire.gather_end(row_go)
    dispatch(0, xa_ref, xown_ref)
    wire.gather_on(other_go, xo_ref)
    wire.gather_on(cot_other, yo_ref)
    down_next = weights_next(2, down_first)
    weights_last(1, up_next)
    wire.gather_end(other_go)
    dispatch(1, xo_ref, xother_ref)
    wire.gather_end(cot_other)
    dispatch(1, yo_ref, yother_ref)
    weights_last(2, down_next)
    keep_wall.wait()
    keep_pick.wait()
    wire.finish()


def forward_call(tokens, packed, cotangent, weights, cos_table, sin_table, table, q_width, k_width, slots):
    groups, few, width = packed.shape
    _, own, part, hidden_units = weights[0].shape
    size = tokens.shape[0]
    seq_len = size * groups
    blocks = k_width // HEAD_DIM * (seq_len // QROWS)
    shape = jax.ShapeDtypeStruct
    vmem = pl.BlockSpec(memory_space=pltpu.VMEM)
    hbm = pl.BlockSpec(memory_space=pl.ANY)
    rows = shape((groups, size, D), narrow)
    count = 80
    picked = shape((own * slots, D), narrow)
    return pl.pallas_call(
        forward_body,
        in_specs=[vmem] * 3 + [hbm] * 3 + [vmem] * 3,
        out_specs=[vmem] * 10 + [hbm] * 12,
        out_shape=[
            shape((seq_len, D), narrow),
            shape((seq_len, q_width), narrow),
            shape((seq_len, k_width), narrow),
            shape((seq_len, k_width), narrow),
            shape((seq_len, q_width), narrow),
            shape((blocks, 1, HEADS // KV_HEADS * QROWS), single),
            shape((size, D), single),
            shape((8, D), single),
            shape((own, 2 * slots, 1), single),
            shape(table.shape, single),
            rows,
            shape((groups, 8, few, width), narrow),
            shape((2, own * slots, seq_len), narrow),
            rows, rows, rows, rows,
            shape((3, 2, 4, own, part, hidden_units), narrow),
            picked, picked, picked, picked,
        ],
        scratch_shapes=[
            pltpu.VMEM((groups, size, D), narrow),
            pltpu.VMEM((groups, 8, few, width), narrow),
            pltpu.VMEM((groups - 1, size, D), narrow),
            pltpu.VMEM((6, size // 2, D), narrow),
            pltpu.VMEM((2, size // 2, D), narrow),
            pltpu.VMEM((size, D), narrow),
            pltpu.VMEM(table.shape, single),
            pltpu.VMEM((2, own * slots, seq_len), narrow),
            pltpu.VMEM((own * slots, D), narrow),
            pltpu.SemaphoreType.DMA((count,)),
            pltpu.SemaphoreType.DMA((count,)),
            pltpu.SemaphoreType.DMA((24,)),
        ],
        compiler_params=pltpu.CompilerParams(collective_id=0, has_side_effects=True),
        cost_estimate=pl.CostEstimate(
            flops=200_000_000_000, bytes_accessed=100_000_000, transcendentals=0
        ),
        name="forward_exchange",
    )(tokens, packed, cotangent, *weights, cos_table, sin_table, table)


def expert_body(
    batch, own_apart, where_ref, all_ref, g_ref, u_ref, d_ref, *refs,
):
    _, halves, rings, _, part, width = all_ref.shape
    pieces = halves * rings
    x_refs, y_refs, w_ref = refs[:batch], refs[batch : 2 * batch], refs[2 * batch]
    refs = refs[2 * batch + 1 :]
    out_refs, row_refs, slot_ref = refs[:batch], refs[batch : 2 * batch], refs[2 * batch]
    gg_ref, gu_ref, gd_ref, held, sems = refs[2 * batch + 1 :]
    half, ring = where_ref[0], where_ref[1]
    e = pl.program_id(0)
    slot = lax.rem(e, 2)

    def each(expert, slot, act):
        for t, own_ref in enumerate((g_ref, u_ref, d_ref)):
            for g in range(halves):
                for r in range(rings):
                    at = g * rings + r
                    target, sem = held.at[slot, t, at], sems.at[slot, t, at]
                    if not own_apart:
                        act(pltpu.make_async_copy(all_ref.at[t, g, r, expert], target, sem))
                        continue
                    own = (half == g) & (ring == r)

                    @pl.when(own)
                    def _():
                        act(pltpu.make_async_copy(own_ref.at[g, expert], target, sem))

                    @pl.when(jnp.logical_not(own))
                    def _():
                        act(pltpu.make_async_copy(all_ref.at[t, g, r, expert], target, sem))

    @pl.when(e == 0)
    def _():
        each(e, slot, lambda copy: copy.start())

    @pl.when(e + 1 < pl.num_programs(0))
    def _():
        each(e + 1, 1 - slot, lambda copy: copy.start())

    for t in range(3):
        for at in range(pieces):
            pltpu.make_async_copy(
                all_ref.at[t, at // rings, at % rings, e], held.at[slot, t, at], sems.at[slot, t, at]
            ).wait()

    def weight(t):
        return held[slot, t].reshape(pieces * part, width)

    def write(ref, value):
        for g in range(halves):
            for r in range(rings):
                at = (g * rings + r) * part
                ref[r ^ ring if own_apart else r, g ^ half, 0] = value[at : at + part].astype(ref.dtype)

    slots = x_refs[0].shape[1]

    def split(outs, value):
        for b, ref in enumerate(outs):
            ref[0] = value[b * slots : (b + 1) * slots].astype(ref.dtype)

    rows = jnp.concatenate([ref[0] for ref in x_refs], axis=0)
    cots = jnp.concatenate([ref[0] for ref in y_refs], axis=0)
    share = w_ref[0]
    gate, up, down = weight(0), weight(1), weight(2)
    gate_pre = dot(rows, gate, 1, 0)
    up_pre = dot(rows, up, 1, 0)
    sig = jax.nn.sigmoid(gate_pre)
    mid = (gate_pre * sig * up_pre).astype(narrow)
    expert_out = dot(mid, down, 1, 1)
    cot_float = cots.astype(single)
    slot_ref[0] = jnp.sum(cot_float * expert_out, axis=-1, keepdims=True)
    split(out_refs, expert_out * share)
    out_low = (cot_float * share).astype(narrow)
    mid_grad = dot(out_low, down, 1, 0)
    write(gd_ref, dot(out_low, mid, 0, 0))
    gate_grad = (mid_grad * up_pre * sig * (1.0 + gate_pre * (1.0 - sig))).astype(narrow)
    up_grad = (mid_grad * gate_pre * sig).astype(narrow)
    split(row_refs, dot(gate_grad, gate, 1, 1) + dot(up_grad, up, 1, 1))
    write(gg_ref, dot(rows, gate_grad, 0, 0))
    write(gu_ref, dot(rows, up_grad, 0, 0))


def expert_call(where, gathered, weights, own_apart, rows, cots, share):
    _, halves, rings, own, part, width = gathered.shape
    batch = len(rows)
    _, slots, depth = rows[0].shape
    pieces = halves * rings
    weight_spec = pl.BlockSpec((rings, halves, 1, part, width), lambda e, h: (0, 0, e, 0, 0))
    row_spec = pl.BlockSpec((1, slots, depth), lambda e, h: (e, 0, 0))
    share_spec = pl.BlockSpec((1, batch * slots, 1), lambda e, h: (e, 0, 0))
    shape = jax.ShapeDtypeStruct
    row_shape = shape((own, slots, depth), narrow)
    outs = pl.pallas_call(
        functools.partial(expert_body, batch, own_apart),
        grid_spec=pltpu.PrefetchScalarGridSpec(
            num_scalar_prefetch=1,
            grid=(own,),
            in_specs=[pl.BlockSpec(memory_space=pl.ANY)] * 4
            + [row_spec] * (2 * batch)
            + [share_spec],
            out_specs=[row_spec] * (2 * batch) + [share_spec] + [weight_spec] * 3,
            scratch_shapes=[
                pltpu.VMEM((2, 3, pieces, part, width), narrow),
                pltpu.SemaphoreType.DMA((2, 3, pieces)),
            ],
        ),
        out_shape=[row_shape] * (2 * batch)
        + [shape((own, batch * slots, 1), single)]
        + [shape((rings, halves, own, part, width), narrow)] * 3,
        cost_estimate=pl.CostEstimate(
            flops=9 * 2 * own * batch * slots * depth * width,
            bytes_accessed=12 * own * depth * width + 8 * batch * own * slots * depth,
            transcendentals=0,
        ),
        name="expert_ffn",
    )(where, gathered, *weights, *rows, *cots, share)
    return outs[:batch], outs[batch : 2 * batch], outs[2 * batch], outs[2 * batch + 1 :]


def local(
    halves, rings,
    tokens, mixing_weight, output_weight, norm_gains, expert_gate, expert_up, expert_down,
    gate_logits, routes, fill_order, cotangent,
):
    groups = lax.axis_size("seq")
    column = lax.axis_index("seq")
    half = lax.axis_index("half")
    ring = lax.axis_index("ring")
    paired = halves == 2
    tok_rows = tokens.shape[1]
    seq_len = tok_rows * groups
    capacity = (seq_len * TOP + EXPERTS - 1) // EXPERTS
    local_count = expert_gate.shape[1]
    own_count = local_count // halves
    part = expert_gate.shape[0]
    fsdp_rows = mixing_weight.shape[0]
    q_width = HEADS * HEAD_DIM // groups
    k_width = KV_HEADS * HEAD_DIM // groups
    mix_width = q_width + 2 * k_width
    own_kv = KV_HEADS // groups
    own_heads = HEADS // groups
    group_size = HEADS // KV_HEADS
    score_scale = 1.0 / math.sqrt(HEAD_DIM)
    query_all = HEADS * HEAD_DIM
    key_all = KV_HEADS * HEAD_DIM

    def gather_seq(value):
        parts = [value] + [swap(value, "seq", j, groups) for j in range(1, groups)]
        whole = jnp.zeros((groups,) + value.shape, value.dtype)
        for j, item in enumerate(parts):
            whole = lax.dynamic_update_index_in_dim(whole, item, column ^ j, 0)
        return whole.reshape((seq_len,) + value.shape[1:])

    def scatter_seq(value):
        blocks = value.reshape((groups, tok_rows) + value.shape[1:])
        total = lax.dynamic_index_in_dim(blocks, column, 0, False).astype(single)
        for j in range(1, groups):
            sent = lax.dynamic_index_in_dim(blocks, column ^ j, 0, False).astype(narrow)
            total = total + swap(sent, "seq", j, groups).astype(single)
        return total

    def exchange_seq(blocks):
        whole = lax.dynamic_update_index_in_dim(
            jnp.zeros_like(blocks), lax.dynamic_index_in_dim(blocks, column, 0, False), column, 0
        )
        for j in range(1, groups):
            sent = lax.dynamic_index_in_dim(blocks, column ^ j, 0, False)
            whole = lax.dynamic_update_index_in_dim(
                whole, swap(sent, "seq", j, groups), column ^ j, 0
            )
        return whole

    packed = jnp.concatenate(
        [
            mixing_weight[:, :query_all].reshape(fsdp_rows, groups, q_width),
            mixing_weight[:, query_all : query_all + key_all].reshape(fsdp_rows, groups, k_width),
            mixing_weight[:, query_all + key_all :].reshape(fsdp_rows, groups, k_width),
            output_weight.reshape(fsdp_rows, groups, q_width),
            jnp.broadcast_to(
                jnp.pad(norm_gains, ((0, 0), (0, PAD - 2)))[:, None], (fsdp_rows, groups, PAD)
            ),
        ],
        2,
    ).transpose(1, 0, 2)
    cos_table, sin_table = rotary_tables(jnp.arange(seq_len, dtype=jnp.int32))
    cos_table, sin_table = jnp.tile(cos_table, (1, 2)), jnp.tile(sin_table, (1, 2))
    own_weights = [
        item.transpose(1, 0, 2).reshape(halves, own_count, part, FF)
        for item in (expert_gate, expert_up, expert_down)
    ]
    inputs = tokens[0].astype(single)
    slots = (capacity + 15) // 16 * 16
    if paired:
        table = jnp.concatenate(
            [
                routes[0].astype(single).T,
                gate_logits[0].T,
                jnp.broadcast_to(fill_order[0].astype(single), (8, seq_len)),
            ],
            0,
        )
        (
            normed_low, queries, keys, values, attended, logs, hidden, gains_float, share,
            other_table, tokens_all, packed, pick, _, _, _, _, gathered,
            own_x, other_x, own_y, other_y,
        ) = forward_call(
            tokens[0], packed, cotangent[0], own_weights, cos_table, sin_table, table,
            q_width, k_width, slots,
        )
        tokens_all = tokens_all.reshape(seq_len, D)
        packed = packed.reshape(D, -1)
        mixing_own = packed[:, :mix_width]
        exit_own = packed[:, mix_width : mix_width + q_width]
        seq_rows = [item.reshape(own_count, slots, D) for item in (own_x, other_x)]
        cot_rows = [item.reshape(own_count, slots, D) for item in (own_y, other_y)]
    else:
        packed = exchange_seq(packed)
        packed = lax.all_gather(packed, ("half", "ring"), axis=0, tiled=False)
        packed = packed.transpose(1, 0, 2, 3).reshape(D, -1)
        mixing_own = packed[:, :mix_width]
        exit_own = packed[:, mix_width : mix_width + q_width]
        gains_float = packed[:, mix_width + q_width : mix_width + q_width + 2].astype(single).T
        tokens_all = gather_seq(tokens[0])
        gathered = jnp.stack(
            [lax.all_gather(item[0], "ring", axis=0, tiled=False)[None] for item in own_weights]
        )
        normed_low, queries, keys, values, attended, logs, attn_part = attention_call(
            tokens_all, mixing_own, exit_own, gains_float, cos_table, sin_table
        )
        hidden = inputs + scatter_seq(attn_part)
        scale_two = lax.rsqrt(jnp.mean(hidden * hidden, axis=-1, keepdims=True) + epsilon)
        seq_rows = [gather_seq((hidden * scale_two * gains_float[1]).astype(narrow))]
        cot_rows = [gather_seq(cotangent[0])]

    if not paired:
        pair_routes = routes
        pair_order = fill_order
        pair_gating = softmax_last(gate_logits)
        expert_ids = column * local_count + half * own_count + jnp.arange(own_count, dtype=jnp.int32)
        places = jnp.arange(seq_len, dtype=jnp.int32)
        chosen = (pair_routes[..., None] == expert_ids).astype(single)
        hits = jnp.sum(chosen, axis=2)
        token_weight = jnp.sum(pair_gating[..., None] * chosen, axis=2)
        place_of = jnp.sum(
            jnp.where(pair_order[:, :, None] == places, places[None, :, None], 0), axis=1
        )
        earlier = (place_of[:, None, :] < place_of[:, :, None]).astype(narrow)
        rank = jnp.einsum(
            "btu,bue->bte", earlier, hits.astype(narrow), preferred_element_type=single
        ).astype(jnp.int32)
        kept = (hits > 0) & (rank < capacity)
        flat_place = jnp.where(kept, rank + jnp.arange(own_count, dtype=jnp.int32) * slots, -1)
        flat_ids = jnp.arange(own_count * slots, dtype=jnp.int32)
        filled = flat_place[:, :, 0:1] == flat_ids
        for e in range(1, own_count):
            filled = filled | (flat_place[:, :, e : e + 1] == flat_ids)
        select = filled.astype(narrow)
        batch = select.shape[0]
        match = flat_place[:, :, :, None] == (
            jnp.arange(own_count, dtype=jnp.int32)[:, None] * slots
            + jnp.arange(slots, dtype=jnp.int32)[None, :]
        )
        slot_weight = jnp.sum(jnp.where(match, token_weight[..., None], 0.0), axis=1)
        share = slot_weight.transpose(1, 0, 2).reshape(own_count, batch * slots, 1)

        def dispatch(rows):
            return [
                lax.dot_general(
                    select[b], item, (((0,), (0,)), ((), ())), preferred_element_type=narrow
                ).reshape(own_count, slots, D)
                for b, item in enumerate(rows)
            ]

        def combine(b, values):
            return lax.dot_general(
                select[b],
                values.reshape(own_count * slots, D),
                (((1,), (0,)), ((), ())),
                preferred_element_type=narrow,
            )

        seq_rows, cot_rows = dispatch(seq_rows), dispatch(cot_rows)

    slot_out, slot_back, slot_grad, (gate_term, up_term, down_term) = expert_call(
        jnp.stack([half, ring]), gathered, own_weights, paired,
        seq_rows, cot_rows, share,
    )
    def by_row(total):
        return total.reshape(local_count, part, FF).transpose(1, 0, 2).astype(single)

    if paired:
        flat = (own_count * slots, D)
        (
            projected_grad, normed_part, gain_sums, hidden_grad, layer_output, logits_rows,
            _, _, _, attn_grad_all, c1, c3, zb, own_terms, other_terms,
        ) = backward_call(
            [item.reshape(flat) for item in slot_back], [item.reshape(flat) for item in slot_out],
            pick, (gate_term, up_term, down_term), hidden, gains_float, cotangent[0], packed,
            queries, keys, values, logs, tokens_all, cos_table, sin_table, slot_grad, table,
            other_table,
        )
        logits_rows = logits_rows.T
        tokens_gradient, attn_total, own_last, other_last = final_call(
            normed_part, down_term, c1, zb, attn_grad_all, normed_low, projected_grad, attended,
            gain_sums, gains_float, hidden_grad, tokens[0], fsdp_rows, packed.shape[1],
        )
        tokens_gradient, layer_output = tokens_gradient[None], layer_output[None]

        def expert_gradient(own, other):
            return by_row(
                jnp.stack([jnp.where(half == 0, own, other), jnp.where(half == 0, other, own)])
            )

        gate_gradient = expert_gradient(own_terms[0], other_terms[0])
        up_gradient = expert_gradient(own_terms[1], other_terms[1])
        down_gradient = expert_gradient(own_last, other_last)
    else:
        slot_grad = slot_grad.reshape(own_count, batch, slots).transpose(1, 0, 2)
        weight_grad_tok = jnp.sum(jnp.where(match, slot_grad[:, None], 0.0), axis=3)
        route_part = jnp.sum(weight_grad_tok[:, :, None, :] * chosen, axis=-1)

        def send_routes(value):
            blocks = value.reshape(groups, tok_rows, TOP)
            total = lax.dynamic_index_in_dim(blocks, column, 0, False)
            for j in range(1, groups):
                sent = lax.dynamic_index_in_dim(blocks, column ^ j, 0, False)
                total = total + swap(sent, "seq", j, groups)
            return total

        route_grad = send_routes(route_part[0])
        gating = softmax_last(
            lax.dynamic_slice_in_dim(gate_logits[0], column * tok_rows, tok_rows, 0)
        )
        logits_rows = gating * (route_grad - jnp.sum(gating * route_grad, axis=-1, keepdims=True))

        def ring_sum(term):
            return lax.psum_scatter(term, "ring", scatter_dimension=0, tiled=False)

        normed_two_grad = scatter_seq(combine(0, slot_back[0]))
        gate_gradient, up_gradient, down_gradient = [
            by_row(ring_sum(term)) for term in (gate_term, up_term, down_term)
        ]
        moe_rows = scatter_seq(combine(0, slot_out[0]))
        layer_output = (hidden + moe_rows).astype(narrow)[None]
        back, gain_two_grad = norm_back(normed_two_grad, hidden, gains_float[1])
        hidden_grad = cotangent[0].astype(single) + back
        attn_grad_all = gather_seq(hidden_grad.astype(narrow))
        projected_grad, normed_part, gain_one_grad = attention_back_call(
            attn_grad_all, exit_own, mixing_own, queries, keys, values, logs, tokens_all,
            cos_table, sin_table,
        )
        mixing_term = dot(normed_low, projected_grad, 0, 0)
        output_term = dot(attn_grad_all, attended, 0, 0)
        gains_term = jnp.stack([gain_one_grad[0], gain_two_grad[0]], 1)
        gains_term = jnp.pad(gains_term, ((0, 0), (0, PAD - 2)))
        attn_term = jnp.concatenate([mixing_term, output_term, gains_term], 1).astype(narrow)
        attn_term = attn_term.reshape(groups, halves * rings, fsdp_rows, -1).transpose(1, 0, 2, 3)
        attn_total = lax.psum_scatter(attn_term, ("half", "ring"), scatter_dimension=0, tiled=False)
        attn_total = exchange_seq(attn_total).astype(single)
        back, _ = norm_back(scatter_seq(normed_part), inputs, gains_float[0])
        tokens_gradient = (hidden_grad + back)[None]

    def columns(first, width):
        return attn_total[:, :, first : first + width].transpose(1, 0, 2).reshape(fsdp_rows, -1)

    mixing_gradient = jnp.concatenate(
        [
            columns(0, q_width),
            columns(q_width, k_width),
            columns(q_width + k_width, k_width),
        ],
        1,
    )
    output_gradient = columns(mix_width, q_width)
    gains_gradient = jnp.sum(attn_total[:, :, mix_width + q_width :][:, :, :2], axis=0)

    return (
        layer_output,
        tokens_gradient,
        mixing_gradient,
        output_gradient,
        gains_gradient,
        gate_gradient,
        up_gradient,
        down_gradient,
        logits_rows[None],
    )


def solution(mesh):
    groups, shards = mesh.shape["seq"], mesh.shape["fsdp"]
    halves = 2 if (EXPERTS // groups) % 2 == 0 and (groups, shards) == (4, 8) else 1
    rings = shards // halves
    grid = Mesh(mesh.devices.reshape(groups, halves, rings), ("seq", "half", "ring"))
    fsdp = ("half", "ring")
    every = ("seq", "half", "ring")
    in_specs = (
        P(fsdp, "seq", None),
        P(every, None),
        P(every, None),
        P(every, None),
        P(fsdp, "seq", None),
        P(fsdp, "seq", None),
        P(fsdp, "seq", None),
        P(fsdp, None, None),
        P(fsdp, None, None),
        P(fsdp, None),
        P(fsdp, "seq", None),
    )
    out_specs = (
        P(fsdp, "seq", None),
        P(fsdp, "seq", None),
        P(every, None),
        P(every, None),
        P(every, None),
        P(fsdp, "seq", None),
        P(fsdp, "seq", None),
        P(fsdp, "seq", None),
        P(fsdp, "seq", None),
    )
    return jax.shard_map(
        functools.partial(local, halves, rings),
        mesh=grid,
        in_specs=in_specs,
        out_specs=out_specs,
        check_vma=False,
    )
```

profile of v0, /device:TPU:21, one launch (start us, length us, event | category | flops | bytes accessed | tf_op | source)
XLA Modules:
  0.0 678.7 jit_solution(2058246186962013031)
XLA Ops:
  0.7 0.6 pad_add_fusion.where_ref
  1.3 0.7 convert_element_type.57
  2.0 0.8 copy.48
  2.8 0.8 convert_bitcast_fusion.3
  3.6 1.4 pad_maximum_fusion.6.table_ref
  5.0 0.8 slice_bitcast_fusion.4
  6.4 1.0 copy.39.cos_ref
  7.6 1.0 copy.40.sin_ref
  8.6 273.3 %forward_exchange.1 = (bf16[1024,1536]{1,0:T(8,128)(2,1)}, bf16[1024,384]{1,0:T(8,128)(2,1)}, bf16[1024,128]{1,0:T(8,128)(2,1)}, bf16[1024,128]{1,0:T(8,128)(2,1...) custom-call(bf16[256,1536]{1,0:T(8,128)(2,1)} %bitcast.115, ...), custom_call_target="tpu_custom_call" | custom-call | flops 199999995904 | bytes 100000000 | tf_op jit(solution)/shard_map/forward_exchange/pallas_call | solution.py:990
  282.0 43.5 %expert_ffn.1 = (bf16[5,208,1536]{2,1,0:T(8,128)(2,1)}, bf16[5,208,1536]{2,1,0:T(8,128)(2,1)}, bf16[5,208,1536]{2,1,0:T(8,128)(2,1)}, bf16[5,208,1536]{2,1,0:T(8...) custom-call(s32[2]{0:T(128)} %pad_add_fusion.where_ref, ...), custom_call_target="tpu_custom_call" | custom-call | flops 29444014080 | bytes 72744960 | tf_op jit(solution)/shard_map/expert_ffn/pallas_call | solution.py:1127
  325.5 237.8 %backward_exchange.1 = (bf16[1024,640]{1,0:T(8,128)(2,1)}, bf16[1024,1536]{1,0:T(8,128)(2,1)}, f32[8,1536]{1,0:T(8,128)}, f32[256,1536]{1,0:T(8,128)}, bf16[256,...) custom-call(bf16[1040,1536]{1,0:T(8,128)(2,1)} %bitcast.120, ...), custom_call_target="tpu_custom_call" | custom-call | flops 149999992832 | bytes 100000000 | tf_op jit(solution)/shard_map/backward_exchange/pallas_call | solution.py:430
  563.3 97.5 %final_exchange.1 = (f32[256,1536]{1,0:T(8,128)}, f32[4,48,1152]{2,1,0:T(8,128)}, bf16[5,192,512]{2,1,0:T(8,128)(2,1)}, bf16[5,192,512]{2,1,0:T(8,128)(2,1)}) custom-call(bf16[4,256,1536]{2,1,0:T(8,128)(2,1)} %bitcast.127, bf16[4,2,5,192,512]{4,3,2,1,0:T(8,128)(2,1)} %get-tuple-element.64.gd_ref, bf16[3,2,5,192,512]{4,3,2,1,0:T(8,128)(2,1)} %get-tuple-element.76.c1_ref, ...), custom_call_target="tpu_custom_call" | custom-call | flops 49999998976 | bytes 100000000 | tf_op jit(solution)/shard_map/final_exchange/pallas_call | solution.py:570
  660.9 1.0 slice_reduce_fusion
  661.9 0.6 copy.47
  662.5 1.0 slice_bitcast_fusion.3
  663.5 1.1 slice_bitcast_fusion
  664.6 0.7 copy.56
  665.4 0.8 pad_maximum_fusion.3
  666.4 0.7 copy-done.1
  667.7 2.6 convert_bitcast_fusion
  670.3 2.6 convert_bitcast_fusion.1
  673.1 2.6 convert_bitcast_fusion.2
  675.6 0.9 copy.72
  676.5 1.1 copy.73
  (41 shorter events, 2.4 us)
Async XLA Ops:
  0.6 6.8 %slice-start = ((bf16[48,2560]{1,0:T(8,128)(2,1)}), bf16[48,1536]{1,0:T(8,128)(2,1)S(1)}, s32[]{:S(2)}) async-start(bf16[48,2560]{1,0:T(8,128)(2,1)} %param.12), calls=%async_computation | async-start | bytes 294912 | tf_op jit(solution)/shard_map/slice | solution.py:1209
  0.7 6.9 %copy-start.6 = (bf16[48,1536]{1,0:T(8,128)(2,1)S(1)}, bf16[48,1536]{1,0:T(8,128)(2,1)}, u32[]{:S(2)}) copy-start(bf16[48,1536]{1,0:T(8,128)(2,1)} %param.13) | copy-start | bytes 442372
  7.6 1.1 copy-start.7
  660.8 5.4 copy-start.3
  660.9 5.4 copy-start.4
  664.6 1.8 copy-start
  664.6 2.4 copy-start.1
  673.0 2.6 copy-start.5
  673.0 3.5 copy-start.2
  675.6 2.0 copy-start.8
where the time goes:
time: 688 us; the launch traced here: 679 us
  Pallas kernels  652 us (95%)
  other arithmetic  14.7 us (2%)
  local copies, waits for them, and re-layouts  10.6 us (2%)
    pallas_call x1, Pallas kernels, forward_call(): pl.pallas_call(forward_body, in_specs=[vmem] * 3 + [hbm] * 3 + [vmem] * 3...  273 us
    pallas_call x1, Pallas kernels, backward_call(): pl.pallas_call(backward_body, in_specs=[hbm] * 9 + [vmem] * 13, out_specs...  238 us
    pallas_call x1, Pallas kernels, final_call(): pl.pallas_call(final_body, in_specs=[hbm] * 5 + [vmem] * 7, out_specs=[vm...  97.5 us
    pallas_call x1, Pallas kernels, expert_call(): pl.pallas_call(functools.partial(expert_body, batch, own_apart), grid_spe...  43.5 us

commit v1 on v0

--- a/solution.py
+++ b/solution.py
@@ -192,7 +192,10 @@
             wide(sin_ref[rows], turned),
         ).astype(narrow)
         normed_part = dot(pg_ref[rows], mix_ref, 1, 1)
-        part_ref[rows] = normed_part.astype(narrow)
+        if len(part_ref.shape) == 3:
+            part_ref[at // size] = normed_part.astype(narrow)
+        else:
+            part_ref[rows] = normed_part.astype(narrow)
         values = tok_ref[rows].astype(single)
         inverse = lax.rsqrt(jnp.mean(values * values, axis=-1, keepdims=True) + epsilon)
         gain = gain + jnp.sum(normed_part * (values * inverse), axis=0, keepdims=True)
@@ -214,7 +217,7 @@
     )
 
 
-def totals(wire, t, first, third, zed, buffers, out_send, own_out, half_out):
+def totals(wire, first, third, zed, buffers, out_send, own_out, half_out):
     sources = (first, third, zed)
     for g in (1, 0):
         loads = [wire.near(ref.at[g], buffers.at[i]) for i, ref in enumerate(sources)]
@@ -230,11 +233,12 @@
 
 
 def backward_body(
-    ba_ref, bo_ref, oa_ref, oo_ref, pickall_ref, tokall_ref, gg_ref, gu_ref, gd_ref,
-    hid_ref, gain_ref, cot_ref, wall_ref, q_ref, k_ref, v_ref, log_ref, cos_ref, sin_ref,
+    ba_ref, bo_ref, oa_ref, oo_ref, pickall_ref, tokall_ref, normed_ref, gg_ref, gu_ref, gd_ref,
+    tok_ref, att_ref, hid_ref, gain_ref, cot_ref, wall_ref, q_ref, k_ref, v_ref, log_ref, cos_ref, sin_ref,
     slot_ref, table_ref, otab_ref,
-    pg_ref, part_ref, gsum_ref, hgrad_ref, layer_ref, lgrad_ref,
-    ra_ref, mo_ref, ma_ref, grad_out, c1_ref, c3_ref, zb_ref, own_ref, hx_ref,
+    tgrad_ref, layer_ref, lgrad_ref, attn_ref,
+    ra_ref, mo_ref, ma_ref, c1_ref, c3_ref, zb_ref, own_ref, hx_ref,
+    pg_ref, free, gw, r1, r2, r3, fin, attn_in,
     ag, out_grad, keys_sum, values_sum, land_a, land_b, land_h, land_m, sums, own_rows, buffers, far,
     leave, passed, passing, values, pick, stage, route_own, route_send, land_r, quarters, land_q, logits,
     send, recv, local,
@@ -283,6 +287,10 @@
             stage[j] = combine(j)
         wire.near(stage, target).wait()
 
+    def own_block(source):
+        wire.near(source.at[s], own_rows).wait()
+        return own_rows[...].astype(single)
+
     core_go = []
     for t in range(3):
         core_go.append(
@@ -294,7 +302,6 @@
     fetch(bo_ref, 1)
     combine_out(mo_ref)
     other_go = scatter(mo_ref, land_a)
-    own_rows[0] = stage[s]
     z_go = []
 
     def send_far(t):
@@ -315,7 +322,6 @@
     fetch(ba_ref, 0)
     combine_out(ra_ref)
     own_go = scatter(ra_ref, land_b)
-    own_rows[1] = stage[s]
     scatter_on(other_go, mo_ref, land_a, 0)
 
     own_count = slot_ref.shape[0]
@@ -333,8 +339,7 @@
     route_own[...] = route_rows(0, table_ref)
     fetch(oa_ref, None)
     combine_out(ma_ref)
-    own_rows[3] = stage[s]
-    total = wire.scatter_end(other_go, land_a, own_rows[0].astype(single))
+    total = wire.scatter_end(other_go, land_a, own_block(mo_ref))
     sums[...] = total.astype(narrow)
     half_go = wire.go(sums, land_h, wire.to_half)
     scatter_on(own_go, ra_ref, land_b, 1)
@@ -343,15 +348,14 @@
         wire.leave(k)
     fetch(oo_ref, 1)
     combine_out(mo_ref)
-    own_rows[2] = stage[s]
     route_send[...] = route_rows(1, otab_ref)
     route_go = wire.go(route_send, land_r, wire.to_half)
-    total = wire.scatter_end(own_go, land_b, own_rows[1].astype(single))
+    total = wire.scatter_end(own_go, land_b, own_block(ra_ref))
     wire.come(half_go)
     total = total + land_h[...].astype(single)
     back, gain_two = norm_back(total, hid_ref[...], gain_ref[1:2])
     hidden_grad = cot_ref[...].astype(single) + back
-    hgrad_ref[...] = hidden_grad
+    tgrad_ref[...] = hidden_grad
     ag[s] = hidden_grad.astype(narrow)
     grad_go = wire.gather(ag.at[s], ag)
     wire.come(route_go)
@@ -361,10 +365,15 @@
         logits[j] = table_ref[TOP : 2 * TOP, j * size : (j + 1) * size]
     quarter_go = quarter_sends(quarters, land_q)
 
+    leave_go = []
+
     def finish_term(t):
         wire.come(core_go[t][1], z_go[t])
+        if t >= 2:
+            wire.leave(leave_go[t - 2])
+        leave_go.append(len(wire.remotes))
         totals(
-            wire, t, terms[t].at[0], c1_ref.at[t], zb_ref.at[t], buffers, leave.at[t],
+            wire, terms[t].at[0], c1_ref.at[t], zb_ref.at[t], buffers, leave.at[t % 2],
             own_ref.at[t], hx_ref.at[t],
         )
 
@@ -375,26 +384,62 @@
     load_tok = wire.near(tokall_ref, tok_rows)
     wire.gather_end(grad_go)
     moe_go = scatter(mo_ref, land_a)
-    moe_own_go = scatter(ma_ref, land_b)
-    keep_grad = wire.near(ag, grad_out)
     exit_own = wall_ref[:, mix_width : mix_width + q_width]
     for j in range(groups):
         out_grad[j * size : (j + 1) * size] = dot(ag[j], exit_own, 1, 0).astype(narrow)
     attend_back_rows(out_grad, q_ref, k_ref, v_ref, log_ref, pg_ref, keys_sum, values_sum)
+    load_tok.wait()
+    gain_one = project_back_rows(
+        pg_ref, wall_ref[:, :mix_width], tok_rows, cos_ref, sin_ref, stage, q_width + k_width, size
+    )
+    norm_go = scatter(stage, land_b)
+    load_normed = wire.near(normed_ref, tok_rows)
     for k in other_go[4:] + own_go[4:]:
         wire.leave(k)
     scatter_on(moe_go, mo_ref, land_a, 0)
-    scatter_on(moe_own_go, ma_ref, land_b, 1)
     finish_term(1)
-    load_tok.wait()
-    gain_one = project_back_rows(
-        pg_ref, wall_ref[:, :mix_width], tok_rows, cos_ref, sin_ref, part_ref, q_width + k_width, size
-    )
-    gsum_ref[...] = jnp.concatenate([gain_one, gain_two, jnp.zeros((6, D), single)], axis=0)
-    total = wire.scatter_end(moe_go, land_a, own_rows[2].astype(single))
+    wire.scatter_on(
+        norm_go, land_b,
+        lambda j: stage[s ^ j, pl.ds(0 if j == 2 else middle, middle)].astype(single),
+        passing.at[2],
+    )
+    total = wire.scatter_end(moe_go, land_a, own_block(mo_ref))
+    for j in (1, 2):
+        pl.semaphore_signal(free, inc=1, device_id=wire.to_seq[j], device_id_type=MESH)
     wire.leave(half_go)
     sums[...] = total.astype(narrow)
     moe_half_go = wire.go(sums, land_m, wire.to_half)
+
+    pl.semaphore_wait(free, 2)
+    moe_own_go = scatter(ma_ref, land_a)
+
+    _, shards, few, width = gw.shape
+    f, last = wire.f, mix_width + q_width
+    shape = (groups, shards, few)
+    load_normed.wait()
+    gw[:, :, :, :mix_width] = (
+        dot(tok_rows[...], pg_ref[...], 0, 0).astype(narrow).reshape(shape + (mix_width,))
+    )
+    grads = ag[...].reshape(groups * size, D)
+    gw[:, :, :, mix_width:last] = (
+        dot(grads, att_ref[...], 0, 0).astype(narrow).reshape(shape + (q_width,))
+    )
+    gains = jnp.concatenate([gain_one, gain_two, jnp.zeros((width - last - 2, D), single)], axis=0)
+    gw[:, :, :, last:] = gains.T.astype(narrow).reshape(shape + (width - last,))
+    pair_go = [wire.go(gw.at[:, f ^ (m + 1)], r1.at[m // 2], wire.to_core) for m in (2, 6, 0, 4)]
+    scatter_on(moe_own_go, ma_ref, land_a, 1)
+    total = wire.scatter_end(norm_go, land_b, stage[s].astype(single))
+    back, _ = norm_back(total, tok_ref[...].astype(single), gain_ref[0:1])
+    tgrad_ref[...] += back
+    wire.come(*pair_go)
+
+    def pair_sum(m):
+        return gw[:, f ^ m].astype(single) + r1[m // 2].astype(single)
+
+    gw[:, f ^ 2] = pair_sum(2).astype(narrow)
+    go_2 = wire.go(gw.at[:, f ^ 2], r2.at[0], wire.to_z)
+    gw[:, f ^ 6] = pair_sum(6).astype(narrow)
+    go_6 = wire.go(gw.at[:, f ^ 6], r2.at[1], wire.to_z)
     wire.come(*quarter_go)
     route_grad = quarters[s]
     for j in range(groups - 1):
@@ -403,16 +448,25 @@
     exponent = jnp.exp(top - jnp.max(top, axis=0, keepdims=True))
     gating = exponent / jnp.sum(exponent, axis=0, keepdims=True)
     lgrad_ref[...] = gating * (route_grad - jnp.sum(gating * route_grad, axis=0, keepdims=True))
-    total = wire.scatter_end(moe_own_go, land_b, hid_ref[...] + own_rows[3].astype(single))
+    finish_term(2)
+    total = wire.scatter_end(moe_own_go, land_a, hid_ref[...] + own_block(ma_ref))
     wire.come(moe_half_go)
     layer_ref[...] = (total + land_m[...].astype(single)).astype(narrow)
-    keep_grad.wait()
+    wire.come(go_6)
+    gw[:, f ^ 4] = (pair_sum(4) + r2[1].astype(single)).astype(narrow)
+    go_4 = wire.go(gw.at[:, f ^ 4], r3, wire.to_half)
+    wire.come(go_2, go_4)
+    fin[...] = pair_sum(0) + r2[0].astype(single) + r3[...].astype(single)
+    attn_in[s] = fin[s]
+    last_go = [wire.go(fin.at[s ^ j], attn_in.at[s], wire.to_seq[j]) for j in range(1, groups)]
+    wire.come(*last_go)
+    wire.near(attn_in, attn_ref).wait()
     wire.finish()
 
 
 def backward_call(
     backs, outs, pick, terms, hidden, gains, cot, wall, q, k, v, logs, tokens_all,
-    cos_table, sin_table, slot_grad, table, other_table,
+    cos_table, sin_table, slot_grad, table, other_table, normed, tok, att, few,
 ):
     size = hidden.shape[0]
     seq_len = tokens_all.shape[0]
@@ -423,32 +477,38 @@
     vmem = pl.BlockSpec(memory_space=pltpu.VMEM)
     hbm = pl.BlockSpec(memory_space=pl.ANY)
     block = (groups, size, D)
+    slab = (groups, few, wall.shape[1])
     mix_width = q.shape[1] + 2 * k.shape[1]
     landing = pltpu.VMEM((6, size // 2, D), narrow)
     route = pltpu.VMEM((TOP, seq_len), single)
-    count = 72
+    count = 96
     return pl.pallas_call(
         backward_body,
-        in_specs=[hbm] * 9 + [vmem] * 13,
-        out_specs=[vmem] * 6 + [hbm] * 9,
+        in_specs=[hbm] * 10 + [vmem] * 15,
+        out_specs=[vmem] * 3 + [hbm] * 9,
         out_shape=[
-            shape((seq_len, mix_width), narrow),
-            shape((seq_len, D), narrow),
-            shape((8, D), single),
             shape((size, D), single),
             shape((size, D), narrow),
             shape((TOP, size), single),
-            shape(block, narrow),
+            shape(slab, single),
             shape(block, narrow),
             shape(block, narrow),
             shape(block, narrow),
             shape((3, halves, own, part, width), narrow),
             shape((3, halves, own, part, width), narrow),
             shape((3, halves, own, part, width), narrow),
-            shape((2, own, part, width), narrow),
-            shape((2, own, part, width), narrow),
+            shape((3, own, part, width), narrow),
+            shape((3, own, part, width), narrow),
         ],
         scratch_shapes=[
+            pltpu.VMEM((seq_len, mix_width), narrow),
+            pltpu.SemaphoreType.REGULAR,
+            pltpu.VMEM((groups, 8) + slab[1:], narrow),
+            pltpu.VMEM((4,) + slab, narrow),
+            pltpu.VMEM((2,) + slab, narrow),
+            pltpu.VMEM(slab, narrow),
+            pltpu.VMEM(slab, single),
+            pltpu.VMEM(slab, single),
             pltpu.VMEM(block, narrow),
             pltpu.VMEM(q.shape, narrow),
             pltpu.VMEM((seq_len, HEAD_DIM), single),
@@ -458,12 +518,12 @@
             pltpu.VMEM((size, D), narrow),
             pltpu.VMEM((size, D), narrow),
             pltpu.VMEM((size, D), narrow),
-            pltpu.VMEM((4, size, D), narrow),
+            pltpu.VMEM((size, D), narrow),
             pltpu.VMEM((3, own, part, width), narrow),
             pltpu.VMEM((2, halves, own, part, width), narrow),
             pltpu.VMEM((2, own, part, width), narrow),
             pltpu.VMEM((2, size // 2, D), narrow),
-            pltpu.VMEM((2, 2, size // 2, D), narrow),
+            pltpu.VMEM((3, 2, size // 2, D), narrow),
             pltpu.VMEM((slot_rows, D), narrow),
             pltpu.VMEM((slot_rows, seq_len), narrow),
             pltpu.VMEM(block, narrow),
@@ -485,125 +545,8 @@
         ),
         name="backward_exchange",
     )(
-        *backs, *outs, pick, tokens_all, *terms, hidden, gains, cot, wall, q, k, v, logs,
-        cos_table, sin_table, slot_grad, table, other_table,
-    )
-
-
-def final_body(
-    part_ref, gd_ref, c1_ref, zb_ref, grad_ref,
-    normed_ref, pg_ref, att_ref, gsum_ref, gain_ref, hgrad_ref, tok_ref,
-    tgrad_ref, attn_ref, own_ref, hx_ref,
-    gw, r1, r2, r3, a2, a6, c4, fin, land_a, passed, passing, own_rows, agv, buffers, leave,
-    send, recv, local,
-):
-    wire = Wire(send, recv, local)
-    s, f, groups = wire.s, wire.f, wire.groups
-    _, shards, few, width = gw.shape
-    depth = groups * shards * few
-    wire.meet()
-
-    norm_go = wire.scatter(lambda j: part_ref.at[s ^ j], land_a)
-    load_grad = wire.near(grad_ref, agv)
-    middle = land_a.shape[1]
-    loads = [
-        wire.near(part_ref.at[s], own_rows),
-        wire.near(part_ref.at[s ^ 2, pl.ds(0, middle)], passed.at[0]),
-        wire.near(part_ref.at[s ^ 1, pl.ds(middle, middle)], passed.at[1]),
-    ]
-    totals(
-        wire, 2, gd_ref.at[0], c1_ref.at[2], zb_ref.at[2], buffers, leave, own_ref, hx_ref
-    )
-    mix_width, q_width = pg_ref.shape[1], att_ref.shape[1]
-    last = mix_width + q_width
-    load_grad.wait()
-    shape = (groups, shards, few)
-    gw[:, :, :, :mix_width] = (
-        dot(normed_ref[...], pg_ref[...], 0, 0).astype(narrow).reshape(shape + (mix_width,))
-    )
-    grads = agv[...].reshape(groups * agv.shape[1], D)
-    gw[:, :, :, mix_width:last] = (
-        dot(grads, att_ref[...], 0, 0).astype(narrow).reshape(shape + (q_width,))
-    )
-    gains = jnp.concatenate([gsum_ref[...], jnp.zeros((width - last - 8, D), single)], axis=0)
-    gw[:, :, :, last:] = gains.T.astype(narrow).reshape(shape + (width - last,))
-    core_go = [wire.go(gw.at[:, f ^ (m + 1)], r1.at[m // 2], wire.to_core) for m in (2, 6, 0, 4)]
-    for load in loads:
-        load.wait()
-    wire.scatter_on(
-        norm_go, land_a, lambda j: passed[0 if j == 2 else 1].astype(single), passing
-    )
-    wire.come(*core_go)
-
-    def pair_sum(m):
-        return gw[:, f ^ m].astype(single) + r1[m // 2].astype(single)
-
-    a2[...] = pair_sum(2).astype(narrow)
-    go_2 = wire.go(a2, r2.at[0], wire.to_z)
-    a6[...] = pair_sum(6).astype(narrow)
-    go_6 = wire.go(a6, r2.at[1], wire.to_z)
-    wire.come(go_6)
-    c4[...] = (pair_sum(4) + r2[1].astype(single)).astype(narrow)
-    go_4 = wire.go(c4, r3, wire.to_half)
-    total = wire.scatter_end(norm_go, land_a, own_rows[...].astype(single))
-    back, _ = norm_back(total, tok_ref[...].astype(single), gain_ref[0:1])
-    tgrad_ref[...] = hgrad_ref[...] + back
-    wire.come(go_2, go_4)
-    fin[...] = pair_sum(0) + r2[0].astype(single) + r3[...].astype(single)
-    attn_ref[s] = fin[s]
-    last_go = [wire.go(fin.at[s ^ j], attn_ref.at[s], wire.to_seq[j]) for j in range(1, groups)]
-    wire.finish()
-
-
-def final_call(part, term, c1, zb, grad_all, normed, pg, att, gsum, gains, hgrad, tok, few, width):
-    size = tok.shape[0]
-    seq_len = normed.shape[0]
-    groups = seq_len // size
-    _, halves, own, rows, units = term.shape
-    shape = jax.ShapeDtypeStruct
-    vmem = pl.BlockSpec(memory_space=pltpu.VMEM)
-    hbm = pl.BlockSpec(memory_space=pl.ANY)
-    block = (groups, size, D)
-    slab = (groups, few, width)
-    landing = pltpu.VMEM((6, size // 2, D), narrow)
-    count = 32
-    return pl.pallas_call(
-        final_body,
-        in_specs=[hbm] * 5 + [vmem] * 7,
-        out_specs=[vmem] * 2 + [hbm] * 2,
-        out_shape=[
-            shape((size, D), single),
-            shape(slab, single),
-            shape((own, rows, units), narrow),
-            shape((own, rows, units), narrow),
-        ],
-        scratch_shapes=[
-            pltpu.VMEM((groups, 8, few, width), narrow),
-            pltpu.VMEM((4,) + slab, narrow),
-            pltpu.VMEM((2,) + slab, narrow),
-            pltpu.VMEM(slab, narrow),
-            pltpu.VMEM(slab, narrow),
-            pltpu.VMEM(slab, narrow),
-            pltpu.VMEM(slab, narrow),
-            pltpu.VMEM(slab, single),
-            landing,
-            pltpu.VMEM((2, size // 2, D), narrow),
-            pltpu.VMEM((2, size // 2, D), narrow),
-            pltpu.VMEM((size, D), narrow),
-            pltpu.VMEM(block, narrow),
-            pltpu.VMEM((3, own, rows, units), narrow),
-            pltpu.VMEM((own, rows, units), narrow),
-            pltpu.SemaphoreType.DMA((count,)),
-            pltpu.SemaphoreType.DMA((count,)),
-            pltpu.SemaphoreType.DMA((count,)),
-        ],
-        compiler_params=pltpu.CompilerParams(collective_id=2, has_side_effects=True),
-        cost_estimate=pl.CostEstimate(
-            flops=50_000_000_000, bytes_accessed=100_000_000, transcendentals=0
-        ),
-        name="final_exchange",
-    )(
-        part.reshape(block), term, c1, zb, grad_all, normed, pg, att, gsum, gains, hgrad, tok,
+        *backs, *outs, pick, tokens_all, normed, *terms, tok, att, hidden, gains, cot, wall,
+        q, k, v, logs, cos_table, sin_table, slot_grad, table, other_table,
     )
 
 
@@ -1110,8 +1053,9 @@
     gate_grad = (mid_grad * up_pre * sig * (1.0 + gate_pre * (1.0 - sig))).astype(narrow)
     up_grad = (mid_grad * gate_pre * sig).astype(narrow)
     split(row_refs, dot(gate_grad, gate, 1, 1) + dot(up_grad, up, 1, 1))
-    write(gg_ref, dot(rows, gate_grad, 0, 0))
-    write(gu_ref, dot(rows, up_grad, 0, 0))
+    both = dot(rows, jnp.concatenate([gate_grad, up_grad], axis=1), 0, 0)
+    write(gg_ref, both[:, :width])
+    write(gu_ref, both[:, width:])
 
 
 def expert_call(where, gathered, weights, own_apart, rows, cots, share):
@@ -1325,19 +1269,15 @@
     if paired:
         flat = (own_count * slots, D)
         (
-            projected_grad, normed_part, gain_sums, hidden_grad, layer_output, logits_rows,
-            _, _, _, attn_grad_all, c1, c3, zb, own_terms, other_terms,
+            tokens_gradient, layer_output, logits_rows, attn_total,
+            _, _, _, _, _, _, own_terms, other_terms,
         ) = backward_call(
             [item.reshape(flat) for item in slot_back], [item.reshape(flat) for item in slot_out],
             pick, (gate_term, up_term, down_term), hidden, gains_float, cotangent[0], packed,
             queries, keys, values, logs, tokens_all, cos_table, sin_table, slot_grad, table,
-            other_table,
+            other_table, normed_low, tokens[0], attended, fsdp_rows,
         )
         logits_rows = logits_rows.T
-        tokens_gradient, attn_total, own_last, other_last = final_call(
-            normed_part, down_term, c1, zb, attn_grad_all, normed_low, projected_grad, attended,
-            gain_sums, gains_float, hidden_grad, tokens[0], fsdp_rows, packed.shape[1],
-        )
         tokens_gradient, layer_output = tokens_gradient[None], layer_output[None]
 
         def expert_gradient(own, other):
@@ -1347,7 +1287,7 @@
 
         gate_gradient = expert_gradient(own_terms[0], other_terms[0])
         up_gradient = expert_gradient(own_terms[1], other_terms[1])
-        down_gradient = expert_gradient(own_last, other_last)
+        down_gradient = expert_gradient(own_terms[2], other_terms[2])
     else:
         slot_grad = slot_grad.reshape(own_count, batch, slots).transpose(1, 0, 2)
         weight_grad_tok = jnp.sum(jnp.where(match, slot_grad[:, None], 0.0), axis=3)

time: 688 us -> 675 us (0.981)
  the two profiles are of different devices: /device:TPU:21 before, /device:TPU:0 now
where the time goes in v1:
time: 675 us; the launch traced here: 665 us
  Pallas kernels  637 us (94%)
  other arithmetic  16.5 us (2%)
  local copies, waits for them, and re-layouts  9.93 us (1%)
    pallas_call x1, Pallas kernels, backward_call(): pl.pallas_call(backward_body, in_specs=[hbm] * 10 + [vmem] * 15, out_spec...  320 us
    pallas_call x1, Pallas kernels, forward_call(): pl.pallas_call(forward_body, in_specs=[vmem] * 3 + [hbm] * 3 + [vmem] * 3...  274 us
    pallas_call x1, Pallas kernels, expert_call(): pl.pallas_call(functools.partial(expert_body, batch, own_apart), grid_spe...  43.4 us

profile of v1, /device:TPU:0, one launch (start us, length us, event | category | flops | bytes accessed | tf_op | source)
XLA Modules:
  0.0 665.2 jit_solution(3196349794402829353)
XLA Ops:
  0.7 0.7 pad_add_fusion.where_ref
  1.3 0.7 convert_element_type.57
  2.0 0.8 copy.48
  2.8 0.8 convert_bitcast_fusion.3
  3.6 1.4 pad_maximum_fusion.6.table_ref
  5.0 0.8 slice_bitcast_fusion.4
  6.4 1.0 copy.39.cos_ref
  7.7 1.0 copy.40.sin_ref
  8.7 274.1 %forward_exchange.1 = (bf16[1024,1536]{1,0:T(8,128)(2,1)}, bf16[1024,384]{1,0:T(8,128)(2,1)}, bf16[1024,128]{1,0:T(8,128)(2,1)}, bf16[1024,128]{1,0:T(8,128)(2,1...) custom-call(bf16[256,1536]{1,0:T(8,128)(2,1)} %bitcast.108, ...), custom_call_target="tpu_custom_call" | custom-call | flops 199999995904 | bytes 100000000 | tf_op jit(solution)/shard_map/forward_exchange/pallas_call | solution.py:933
  282.8 43.4 %expert_ffn.1 = (bf16[5,208,1536]{2,1,0:T(8,128)(2,1)}, bf16[5,208,1536]{2,1,0:T(8,128)(2,1)}, bf16[5,208,1536]{2,1,0:T(8,128)(2,1)}, bf16[5,208,1536]{2,1,0:T(8...) custom-call(s32[2]{0:T(128)} %pad_add_fusion.where_ref, ...), custom_call_target="tpu_custom_call" | custom-call | flops 29444014080 | bytes 72744960 | tf_op jit(solution)/shard_map/expert_ffn/pallas_call | solution.py:1071
  326.2 320.0 %backward_exchange.1 = (f32[256,1536]{1,0:T(8,128)}, bf16[256,1536]{1,0:T(8,128)(2,1)}, f32[8,256]{1,0:T(8,128)}, f32[4,48,1152]{2,1,0:T(8,128)}, bf16[4,256,153...) custom-call(bf16[1040,1536]{1,0:T(8,128)(2,1)} %bitcast.115, ...), custom_call_target="tpu_custom_call" | custom-call | flops 149999992832 | bytes 100000000 | tf_op jit(solution)/shard_map/backward_exchange/pallas_call | solution.py:485
  646.2 1.1 slice_reduce_fusion
  647.3 0.6 copy.47
  647.9 1.0 slice_bitcast_fusion.3
  648.9 1.1 slice_bitcast_fusion
  650.0 0.7 copy.56
  650.7 0.8 pad_maximum_fusion.3
  651.6 2.2 broadcast_select_fusion.1
  653.9 2.6 convert_bitcast_fusion
  656.7 2.6 convert_bitcast_fusion.2
  659.5 2.6 convert_bitcast_fusion.1
  662.1 0.9 copy.72
  663.0 1.1 copy.73
  664.1 0.6 copy.74
  (33 shorter events, 1.4 us)
Async XLA Ops:
  0.6 6.8 %slice-start = ((bf16[48,2560]{1,0:T(8,128)(2,1)}), bf16[48,1536]{1,0:T(8,128)(2,1)S(1)}, s32[]{:S(2)}) async-start(bf16[48,2560]{1,0:T(8,128)(2,1)} %param.12), calls=%async_computation | async-start | bytes 294912 | tf_op jit(solution)/shard_map/slice | solution.py:1153
  0.7 6.9 %copy-start.3 = (bf16[48,1536]{1,0:T(8,128)(2,1)S(1)}, bf16[48,1536]{1,0:T(8,128)(2,1)}, u32[]{:S(2)}) copy-start(bf16[48,1536]{1,0:T(8,128)(2,1)} %param.13) | copy-start | bytes 442372
  7.6 1.1 copy-start.4
  646.2 5.4 copy-start
  659.5 2.6 copy-start.2
  659.5 3.5 copy-start.1
  662.1 2.0 copy-start.5

commit v2 on v1

--- a/solution.py
+++ b/solution.py
@@ -217,7 +217,7 @@
     )
 
 
-def totals(wire, first, third, zed, buffers, out_send, own_out, half_out):
+def totals(wire, begin, first, third, zed, buffers, out_send, own_out, half_out):
     sources = (first, third, zed)
     for g in (1, 0):
         loads = [wire.near(ref.at[g], buffers.at[i]) for i, ref in enumerate(sources)]
@@ -226,7 +226,8 @@
         total = buffers[0].astype(single) + buffers[1].astype(single) + buffers[2].astype(single)
         if g:
             out_send[...] = total.astype(narrow)
-            wire.go(out_send, half_out, wire.to_half)
+            key = wire.plan(out_send, half_out, wire.to_half)
+            begin(key)
         else:
             buffers[0] = total.astype(narrow)
             wire.near(buffers.at[0], own_out).wait()
@@ -307,7 +308,9 @@
     def send_far(t):
         wire.come(core_go[t][0])
         if t >= 2:
-            wire.leave(z_go[t - 2])
+            for k in z_go[t - 2]:
+                wire.leave(k)
+        z_go.append([])
         for g in (1, 0):
             loads = [
                 wire.near(terms[t].at[2, g], buffers.at[0]),
@@ -316,7 +319,7 @@
             for load in loads:
                 load.wait()
             far[t % 2, g] = (buffers[0].astype(single) + buffers[1].astype(single)).astype(narrow)
-        z_go.append(wire.go(far.at[t % 2], zb_ref.at[t], wire.to_z))
+            z_go[t].append(wire.go(far.at[t % 2, g], zb_ref.at[t, g], wire.to_z))
 
     send_far(0)
     fetch(ba_ref, 0)
@@ -367,17 +370,20 @@
 
     leave_go = []
 
-    def finish_term(t):
-        wire.come(core_go[t][1], z_go[t])
+    def now(k):
+        wire.remotes[k].start()
+
+    def finish_term(t, begin):
+        wire.come(core_go[t][1], *z_go[t])
         if t >= 2:
             wire.leave(leave_go[t - 2])
         leave_go.append(len(wire.remotes))
         totals(
-            wire, terms[t].at[0], c1_ref.at[t], zb_ref.at[t], buffers, leave.at[t % 2],
+            wire, begin, terms[t].at[0], c1_ref.at[t], zb_ref.at[t], buffers, leave.at[t % 2],
             own_ref.at[t], hx_ref.at[t],
         )
 
-    finish_term(0)
+    finish_term(0, now)
     wire.gather_on(grad_go, ag)
     send_far(2)
     tok_rows = values.at[pl.ds(0, groups * size)]
@@ -397,7 +403,7 @@
     for k in other_go[4:] + own_go[4:]:
         wire.leave(k)
     scatter_on(moe_go, mo_ref, land_a, 0)
-    finish_term(1)
+    finish_term(1, now)
     wire.scatter_on(
         norm_go, land_b,
         lambda j: stage[s ^ j, pl.ds(0 if j == 2 else middle, middle)].astype(single),
@@ -448,13 +454,15 @@
     exponent = jnp.exp(top - jnp.max(top, axis=0, keepdims=True))
     gating = exponent / jnp.sum(exponent, axis=0, keepdims=True)
     lgrad_ref[...] = gating * (route_grad - jnp.sum(gating * route_grad, axis=0, keepdims=True))
-    finish_term(2)
+    held = []
+    finish_term(2, held.append)
     total = wire.scatter_end(moe_own_go, land_a, hid_ref[...] + own_block(ma_ref))
     wire.come(moe_half_go)
     layer_ref[...] = (total + land_m[...].astype(single)).astype(narrow)
     wire.come(go_6)
     gw[:, f ^ 4] = (pair_sum(4) + r2[1].astype(single)).astype(narrow)
     go_4 = wire.go(gw.at[:, f ^ 4], r3, wire.to_half)
+    now(held[0])
     wire.come(go_2, go_4)
     fin[...] = pair_sum(0) + r2[0].astype(single) + r3[...].astype(single)
     attn_in[s] = fin[s]
@@ -633,41 +641,34 @@
         pl.semaphore_wait(barrier, len(peers))
 
     def go(self, source, target, peer):
+        k = self.plan(source, target, peer)
+        self.remotes[k].start()
+        return k
+
+    def plan(self, source, target, peer):
         k = len(self.remotes)
-        copy = pltpu.make_async_remote_copy(
-            src_ref=source, dst_ref=target, send_sem=self.send.at[k], recv_sem=self.recv.at[k],
-            device_id=peer, device_id_type=MESH,
-        )
-        copy.start()
-        self.remotes.append(copy)
+        self.remotes.append(
+            pltpu.make_async_remote_copy(
+                src_ref=source, dst_ref=target, send_sem=self.send.at[k],
+                recv_sem=self.recv.at[k], device_id=peer, device_id_type=MESH,
+            )
+        )
         self.landed.append(False)
         self.left.append(False)
         return k
 
     def by_core(self, *sends):
-        keys = []
-        made = []
-        for source, target, peer in sends:
-            k = len(self.remotes)
-            copy = pltpu.make_async_remote_copy(
-                src_ref=source, dst_ref=target, send_sem=self.send.at[k],
-                recv_sem=self.recv.at[k], device_id=peer, device_id_type=MESH,
-            )
-            self.remotes.append(copy)
-            self.landed.append(False)
-            self.left.append(False)
-            keys.append(k)
-            made.append(copy)
+        keys = [self.plan(*send) for send in sends]
 
         @pl.when(self.r % 2 == 0)
         def _():
-            for copy in made:
-                copy.start()
+            for k in keys:
+                self.remotes[k].start()
 
         @pl.when(self.r % 2 == 1)
         def _():
-            for copy in reversed(made):
-                copy.start()
+            for k in reversed(keys):
+                self.remotes[k].start()
 
         return keys
 

time: 675 us -> 669 us (level)
  no operation moved by 1% of the time
where the time goes in v2:
time: 669 us; the launch traced here: 659 us
  Pallas kernels  631 us (94%)
  other arithmetic  16.5 us (2%)
  local copies, waits for them, and re-layouts  9.93 us (1%)
    pallas_call x1, Pallas kernels, backward_call(): pl.pallas_call(backward_body, in_specs=[hbm] * 10 + [vmem] * 15, out_spec...  313 us
    pallas_call x1, Pallas kernels, forward_call(): pl.pallas_call(forward_body, in_specs=[vmem] * 3 + [hbm] * 3 + [vmem] * 3...  274 us
    pallas_call x1, Pallas kernels, expert_call(): pl.pallas_call(functools.partial(expert_body, batch, own_apart), grid_spe...  43.4 us

profile of v2, /device:TPU:0, one launch (start us, length us, event | category | flops | bytes accessed | tf_op | source)
XLA Modules:
  0.0 658.7 jit_solution(7008278989940449841)
XLA Ops:
  0.7 0.7 pad_add_fusion.where_ref
  1.3 0.7 convert_element_type.57
  2.0 0.8 copy.48
  2.8 0.8 convert_bitcast_fusion.3
  3.6 1.4 pad_maximum_fusion.6.table_ref
  5.0 0.8 slice_bitcast_fusion.4
  6.4 1.0 copy.39.cos_ref
  7.7 1.0 copy.40.sin_ref
  8.7 274.1 %forward_exchange.1 = (bf16[1024,1536]{1,0:T(8,128)(2,1)}, bf16[1024,384]{1,0:T(8,128)(2,1)}, bf16[1024,128]{1,0:T(8,128)(2,1)}, bf16[1024,128]{1,0:T(8,128)(2,1...) custom-call(bf16[256,1536]{1,0:T(8,128)(2,1)} %bitcast.108, ...), custom_call_target="tpu_custom_call" | custom-call | flops 199999995904 | bytes 100000000 | tf_op jit(solution)/shard_map/forward_exchange/pallas_call | solution.py:934
  282.8 43.4 %expert_ffn.1 = (bf16[5,208,1536]{2,1,0:T(8,128)(2,1)}, bf16[5,208,1536]{2,1,0:T(8,128)(2,1)}, bf16[5,208,1536]{2,1,0:T(8,128)(2,1)}, bf16[5,208,1536]{2,1,0:T(8...) custom-call(s32[2]{0:T(128)} %pad_add_fusion.where_ref, ...), custom_call_target="tpu_custom_call" | custom-call | flops 29444014080 | bytes 72744960 | tf_op jit(solution)/shard_map/expert_ffn/pallas_call | solution.py:1072
  326.2 313.5 %backward_exchange.1 = (f32[256,1536]{1,0:T(8,128)}, bf16[256,1536]{1,0:T(8,128)(2,1)}, f32[8,256]{1,0:T(8,128)}, f32[4,48,1152]{2,1,0:T(8,128)}, bf16[4,256,153...) custom-call(bf16[1040,1536]{1,0:T(8,128)(2,1)} %bitcast.115, ...), custom_call_target="tpu_custom_call" | custom-call | flops 149999992832 | bytes 100000000 | tf_op jit(solution)/shard_map/backward_exchange/pallas_call | solution.py:493
  639.7 1.1 slice_reduce_fusion
  640.8 0.6 copy.47
  641.4 1.0 slice_bitcast_fusion.3
  642.4 1.1 slice_bitcast_fusion
  643.5 0.7 copy.56
  644.3 0.8 pad_maximum_fusion.3
  645.1 2.2 broadcast_select_fusion.1
  647.4 2.6 convert_bitcast_fusion
  650.2 2.6 convert_bitcast_fusion.2
  653.0 2.6 convert_bitcast_fusion.1
  655.6 0.9 copy.72
  656.5 1.1 copy.73
  657.6 0.6 copy.74
  (33 shorter events, 1.4 us)
Async XLA Ops:
  0.6 6.8 %slice-start = ((bf16[48,2560]{1,0:T(8,128)(2,1)}), bf16[48,1536]{1,0:T(8,128)(2,1)S(1)}, s32[]{:S(2)}) async-start(bf16[48,2560]{1,0:T(8,128)(2,1)} %param.12), calls=%async_computation | async-start | bytes 294912 | tf_op jit(solution)/shard_map/slice | solution.py:1154
  0.7 6.9 %copy-start.3 = (bf16[48,1536]{1,0:T(8,128)(2,1)S(1)}, bf16[48,1536]{1,0:T(8,128)(2,1)}, u32[]{:S(2)}) copy-start(bf16[48,1536]{1,0:T(8,128)(2,1)} %param.13) | copy-start | bytes 442372
  7.6 1.1 copy-start.4
  639.7 5.4 copy-start
  653.0 2.6 copy-start.2
  653.0 3.5 copy-start.1
  655.6 2.0 copy-start.5

commit v3 on v2

--- a/solution.py
+++ b/solution.py
@@ -300,18 +300,16 @@
                 wire.go(terms[t].at[1], c1_ref.at[t], wire.to_core),
             )
         )
-    fetch(bo_ref, 1)
-    combine_out(mo_ref)
-    other_go = scatter(mo_ref, land_a)
     z_go = []
 
-    def send_far(t):
-        wire.come(core_go[t][0])
+    def send_far(t, which=(1, 0)):
+        if which[0]:
+            wire.come(core_go[t][0])
+            z_go.append([])
         if t >= 2:
             for k in z_go[t - 2]:
                 wire.leave(k)
-        z_go.append([])
-        for g in (1, 0):
+        for g in which:
             loads = [
                 wire.near(terms[t].at[2, g], buffers.at[0]),
                 wire.near(c3_ref.at[t, g], buffers.at[1]),
@@ -321,7 +319,11 @@
             far[t % 2, g] = (buffers[0].astype(single) + buffers[1].astype(single)).astype(narrow)
             z_go[t].append(wire.go(far.at[t % 2, g], zb_ref.at[t, g], wire.to_z))
 
-    send_far(0)
+    send_far(0, (1,))
+    fetch(bo_ref, 1)
+    combine_out(mo_ref)
+    other_go = scatter(mo_ref, land_a)
+    send_far(0, (0,))
     fetch(ba_ref, 0)
     combine_out(ra_ref)
     own_go = scatter(ra_ref, land_b)

time: 669 us -> 675 us (level)
  no operation moved by 1% of the time
where the time goes in v3:
time: 675 us; the launch traced here: 665 us
  Pallas kernels  637 us (94%)
  other arithmetic  16.5 us (2%)
  local copies, waits for them, and re-layouts  9.93 us (1%)
    pallas_call x1, Pallas kernels, backward_call(): pl.pallas_call(backward_body, in_specs=[hbm] * 10 + [vmem] * 15, out_spec...  319 us
    pallas_call x1, Pallas kernels, forward_call(): pl.pallas_call(forward_body, in_specs=[vmem] * 3 + [hbm] * 3 + [vmem] * 3...  274 us
    pallas_call x1, Pallas kernels, expert_call(): pl.pallas_call(functools.partial(expert_body, batch, own_apart), grid_spe...  43.4 us

profile of v3, /device:TPU:0, one launch (start us, length us, event | category | flops | bytes accessed | tf_op | source)
XLA Modules:
  0.0 664.5 jit_solution(8477922750272718212)
XLA Ops:
  0.7 0.7 pad_add_fusion.where_ref
  1.3 0.7 convert_element_type.57
  2.0 0.8 copy.48
  2.8 0.8 convert_bitcast_fusion.3
  3.6 1.4 pad_maximum_fusion.6.table_ref
  5.0 0.8 slice_bitcast_fusion.4
  6.4 1.0 copy.39.cos_ref
  7.7 1.0 copy.40.sin_ref
  8.7 274.1 %forward_exchange.1 = (bf16[1024,1536]{1,0:T(8,128)(2,1)}, bf16[1024,384]{1,0:T(8,128)(2,1)}, bf16[1024,128]{1,0:T(8,128)(2,1)}, bf16[1024,128]{1,0:T(8,128)(2,1...) custom-call(bf16[256,1536]{1,0:T(8,128)(2,1)} %bitcast.108, ...), custom_call_target="tpu_custom_call" | custom-call | flops 199999995904 | bytes 100000000 | tf_op jit(solution)/shard_map/forward_exchange/pallas_call | solution.py:936
  282.8 43.4 %expert_ffn.1 = (bf16[5,208,1536]{2,1,0:T(8,128)(2,1)}, bf16[5,208,1536]{2,1,0:T(8,128)(2,1)}, bf16[5,208,1536]{2,1,0:T(8,128)(2,1)}, bf16[5,208,1536]{2,1,0:T(8...) custom-call(s32[2]{0:T(128)} %pad_add_fusion.where_ref, ...), custom_call_target="tpu_custom_call" | custom-call | flops 29444014080 | bytes 72744960 | tf_op jit(solution)/shard_map/expert_ffn/pallas_call | solution.py:1074
  326.2 319.4 %backward_exchange.1 = (f32[256,1536]{1,0:T(8,128)}, bf16[256,1536]{1,0:T(8,128)(2,1)}, f32[8,256]{1,0:T(8,128)}, f32[4,48,1152]{2,1,0:T(8,128)}, bf16[4,256,153...) custom-call(bf16[1040,1536]{1,0:T(8,128)(2,1)} %bitcast.115, ...), custom_call_target="tpu_custom_call" | custom-call | flops 149999992832 | bytes 100000000 | tf_op jit(solution)/shard_map/backward_exchange/pallas_call | solution.py:495
  645.6 1.1 slice_reduce_fusion
  646.6 0.6 copy.47
  647.3 1.0 slice_bitcast_fusion.3
  648.2 1.1 slice_bitcast_fusion
  649.3 0.7 copy.56
  650.1 0.8 pad_maximum_fusion.3
  650.9 2.2 broadcast_select_fusion.1
  653.3 2.6 convert_bitcast_fusion
  656.1 2.6 convert_bitcast_fusion.2
  658.9 2.6 convert_bitcast_fusion.1
  661.5 0.9 copy.72
  662.3 1.1 copy.73
  663.5 0.6 copy.74
  (33 shorter events, 1.4 us)
Async XLA Ops:
  0.6 6.8 %slice-start = ((bf16[48,2560]{1,0:T(8,128)(2,1)}), bf16[48,1536]{1,0:T(8,128)(2,1)S(1)}, s32[]{:S(2)}) async-start(bf16[48,2560]{1,0:T(8,128)(2,1)} %param.12), calls=%async_computation | async-start | bytes 294912 | tf_op jit(solution)/shard_map/slice | solution.py:1156
  0.7 6.9 %copy-start.3 = (bf16[48,1536]{1,0:T(8,128)(2,1)S(1)}, bf16[48,1536]{1,0:T(8,128)(2,1)}, u32[]{:S(2)}) copy-start(bf16[48,1536]{1,0:T(8,128)(2,1)} %param.13) | copy-start | bytes 442372
  7.6 1.1 copy-start.4
  645.6 5.4 copy-start
  658.9 2.6 copy-start.2
  658.9 3.5 copy-start.1
  661.5 2.0 copy-start.5

commit v4 on v2

--- a/solution.py
+++ b/solution.py
@@ -340,13 +340,13 @@
         return total
 
     route_own[...] = route_rows(0, table_ref)
-    fetch(oa_ref, None)
-    combine_out(ma_ref)
     total = wire.scatter_end(other_go, land_a, own_block(mo_ref))
     sums[...] = total.astype(narrow)
     half_go = wire.go(sums, land_h, wire.to_half)
     scatter_on(own_go, ra_ref, land_b, 1)
     send_far(1)
+    fetch(oa_ref, None)
+    combine_out(ma_ref)
     for k in other_go:
         wire.leave(k)
     fetch(oo_ref, 1)

time: 669 us -> 669 us (level)
  no operation moved by 1% of the time
where the time goes in v4:
time: 669 us; the launch traced here: 659 us
  Pallas kernels  631 us (94%)
  other arithmetic  16.5 us (2%)
  local copies, waits for them, and re-layouts  9.93 us (1%)
    pallas_call x1, Pallas kernels, backward_call(): pl.pallas_call(backward_body, in_specs=[hbm] * 10 + [vmem] * 15, out_spec...  313 us
    pallas_call x1, Pallas kernels, forward_call(): pl.pallas_call(forward_body, in_specs=[vmem] * 3 + [hbm] * 3 + [vmem] * 3...  274 us
    pallas_call x1, Pallas kernels, expert_call(): pl.pallas_call(functools.partial(expert_body, batch, own_apart), grid_spe...  43.4 us

profile of v4, /device:TPU:0, one launch (start us, length us, event | category | flops | bytes accessed | tf_op | source)
XLA Modules:
  0.0 658.7 jit_solution(3712630444074557833)
XLA Ops:
  0.7 0.7 pad_add_fusion.where_ref
  1.3 0.7 convert_element_type.57
  2.0 0.8 copy.48
  2.8 0.8 convert_bitcast_fusion.3
  3.6 1.4 pad_maximum_fusion.6.table_ref
  5.0 0.8 slice_bitcast_fusion.4
  6.4 1.0 copy.39.cos_ref
  7.7 1.0 copy.40.sin_ref
  8.7 274.1 %forward_exchange.1 = (bf16[1024,1536]{1,0:T(8,128)(2,1)}, bf16[1024,384]{1,0:T(8,128)(2,1)}, bf16[1024,128]{1,0:T(8,128)(2,1)}, bf16[1024,128]{1,0:T(8,128)(2,1...) custom-call(bf16[256,1536]{1,0:T(8,128)(2,1)} %bitcast.108, ...), custom_call_target="tpu_custom_call" | custom-call | flops 199999995904 | bytes 100000000 | tf_op jit(solution)/shard_map/forward_exchange/pallas_call | solution.py:934
  282.8 43.4 %expert_ffn.1 = (bf16[5,208,1536]{2,1,0:T(8,128)(2,1)}, bf16[5,208,1536]{2,1,0:T(8,128)(2,1)}, bf16[5,208,1536]{2,1,0:T(8,128)(2,1)}, bf16[5,208,1536]{2,1,0:T(8...) custom-call(s32[2]{0:T(128)} %pad_add_fusion.where_ref, ...), custom_call_target="tpu_custom_call" | custom-call | flops 29444014080 | bytes 72744960 | tf_op jit(solution)/shard_map/expert_ffn/pallas_call | solution.py:1072
  326.2 313.5 %backward_exchange.1 = (f32[256,1536]{1,0:T(8,128)}, bf16[256,1536]{1,0:T(8,128)(2,1)}, f32[8,256]{1,0:T(8,128)}, f32[4,48,1152]{2,1,0:T(8,128)}, bf16[4,256,153...) custom-call(bf16[1040,1536]{1,0:T(8,128)(2,1)} %bitcast.115, ...), custom_call_target="tpu_custom_call" | custom-call | flops 149999992832 | bytes 100000000 | tf_op jit(solution)/shard_map/backward_exchange/pallas_call | solution.py:493
  639.7 1.1 slice_reduce_fusion
  640.8 0.6 copy.47
  641.4 1.0 slice_bitcast_fusion.3
  642.4 1.1 slice_bitcast_fusion
  643.5 0.7 copy.56
  644.3 0.8 pad_maximum_fusion.3
  645.1 2.2 broadcast_select_fusion.1
  647.4 2.6 convert_bitcast_fusion
  650.2 2.6 convert_bitcast_fusion.2
  653.0 2.6 convert_bitcast_fusion.1
  655.6 0.9 copy.72
  656.5 1.1 copy.73
  657.6 0.6 copy.74
  (33 shorter events, 1.4 us)
Async XLA Ops:
  0.6 6.8 %slice-start = ((bf16[48,2560]{1,0:T(8,128)(2,1)}), bf16[48,1536]{1,0:T(8,128)(2,1)S(1)}, s32[]{:S(2)}) async-start(bf16[48,2560]{1,0:T(8,128)(2,1)} %param.12), calls=%async_computation | async-start | bytes 294912 | tf_op jit(solution)/shard_map/slice | solution.py:1154
  0.7 6.9 %copy-start.3 = (bf16[48,1536]{1,0:T(8,128)(2,1)S(1)}, bf16[48,1536]{1,0:T(8,128)(2,1)}, u32[]{:S(2)}) copy-start(bf16[48,1536]{1,0:T(8,128)(2,1)} %param.13) | copy-start | bytes 442372
  7.6 1.1 copy-start.4
  639.7 5.4 copy-start
  653.0 2.6 copy-start.2
  653.0 3.5 copy-start.1
  655.6 2.0 copy-start.5
